TPU v7x, 32 devices: a whole 2x2x4 slice. The times are simulated.
32 devices in a mesh: wide: 16 (over z, x, core), narrow: 2 (over y).
Axes of the slice: x: 2, y: 2, z: 4, core: 2. Of those that a mesh axis runs over, the one named last changes fastest.
Arguments:
- tokens: bfloat16 [16384, 512], P(('wide', 'narrow')), may hold values from -6 to 6
- input_weight: bfloat16 [2, 512, 3, 512], P(None, None, None, 'narrow'), may hold values from -0.25 to 0.25
- query_bias: float32 [2, 512], P(None, 'narrow'), may hold values from -4 to 4
- value_bias: float32 [2, 512], P(None, 'narrow'), may hold values from -0.5 to 0.5
- output_weight: bfloat16 [2, 512, 512], P(None, 'narrow'), may hold values from -4 to 4
- output_bias: float32 [2, 512], replicated, may hold values from -3 to 3
- first_gain: float32 [2, 512], replicated, may hold values from 0.5 to 1.5
- first_shift: float32 [2, 512], replicated, may hold values from -3 to 3
- expand_weight: bfloat16 [2, 512, 2048], P(None, None, 'narrow'), may hold values from -0.25 to 0.25
- expand_bias: float32 [2, 2048], P(None, 'narrow'), may hold values from -3 to 3
- shrink_weight: bfloat16 [2, 2048, 512], P(None, 'narrow'), may hold values from -0.125 to 0.125
- shrink_bias: float32 [2, 512], replicated, may hold values from -3 to 3
- second_gain: float32 [2, 512], replicated, may hold values from 0.5 to 1.5
- second_shift: float32 [2, 512], replicated, may hold values from -3 to 3
- lengths: int32 [32], P('wide'), may hold values from 0 to 1024, as said below
- bucket: int32 [16], P('wide'), may hold values from 0 to 1, as said below
- cotangent: bfloat16 [16384, 512], P(('wide', 'narrow')), may hold values from -6 to 6
Outputs:
- layer_output: float32 [16384, 512], P(('wide', 'narrow'))
- input_grad: float32 [16384, 512], P(('wide', 'narrow'))
- input_weight_grad: float32 [2, 512, 3, 512], P(None, None, None, 'narrow')
- query_bias_grad: float32 [2, 512], P(None, 'narrow')
- value_bias_grad: float32 [2, 512], P(None, 'narrow')
- output_weight_grad: float32 [2, 512, 512], P(None, 'narrow')
- output_bias_grad: float32 [2, 512], replicated
- first_gain_grad: float32 [2, 512], replicated
- first_shift_grad: float32 [2, 512], replicated
- expand_weight_grad: float32 [2, 512, 2048], P(None, None, 'narrow')
- expand_bias_grad: float32 [2, 2048], P(None, 'narrow')
- shrink_weight_grad: float32 [2, 2048, 512], P(None, 'narrow')
- shrink_bias_grad: float32 [2, 512], replicated
- second_gain_grad: float32 [2, 512], replicated
- second_shift_grad: float32 [2, 512], replicated
Inputs may be any that keep to these rules, and one draw needn't show every extreme that they name: Entries 2 i and 2 i + 1 are the lengths of the sequences of index i of wide: either 1024 and 0 or half of 1024 twice; exactly half of the indices hold a single sequence. `bucket`: 0 where index i of wide holds one sequence of 1024 tokens, 1 where it holds two of half that length; agrees with lengths.
All inputs are finite; a program needn't handle non-finite values.
Results may differ from a plain program's by a relative error of at most 0.025.
Values may be sent and summed in bfloat16 or wider, within the bound.
A program may use at most 128 MiB of HBM per device.

v0:
```python
import functools

import jax
import jax.numpy as jnp
from jax import lax
from jax.experimental import pallas as pl
from jax.experimental.pallas import tpu as pltpu
from jax.sharding import PartitionSpec as P

DH = 64
EPSILON = 1e-12
MASKED = -1e9
AXES = ("wide", "narrow")
F32 = jnp.float32
BF16 = jnp.bfloat16
STATES = 17


def dot(a, b):
    return lax.dot_general(a, b, (((1,), (0,)), ((), ())), preferred_element_type=F32)


def dot_rt(a, b):
    return lax.dot_general(a, b, (((1,), (1,)), ((), ())), preferred_element_type=F32)


def dot_lt(a, b):
    return lax.dot_general(a, b, (((0,), (0,)), ((), ())), preferred_element_type=F32)


def lane_halves(shape):
    lane = lax.broadcasted_iota(jnp.int32, shape, len(shape) - 1)
    return lane < DH


def normalise(x):
    centre = x - jnp.mean(x, -1, keepdims=True)
    scale = lax.rsqrt(jnp.mean(centre * centre, -1, keepdims=True) + EPSILON)
    return centre * scale, scale


def gelu_parts(a):
    square = jnp.exp(-0.5 * a * a)
    size = jnp.abs(a)
    t = 1.0 / (1.0 + (0.3275911 * 0.7071067811865476) * size)
    poly = t * (
        0.127414796
        + t * (-0.142248368 + t * (0.7107068705 + t * (-0.7265760135 + t * 0.5307027145)))
    )
    tail = poly * square
    phi = jnp.where(a >= 0, 1.0 - tail, tail)
    return a * phi, phi + a * square * 0.3989422804014327


def ring_size(chips):
    return min(chips, 8)


class Links:
    def __init__(self):
        self.wide, self.narrow = lax.axis_index("wide"), lax.axis_index("narrow")
        self.core = lax.rem(self.wide, 2)
        self.chip = self.wide // 2
        self.bit = lax.rem(self.chip, 2)
        other_core, other_narrow = self.wide + 1 - 2 * self.core, 1 - self.narrow
        self.beside = (other_core, self.narrow)
        self.across = (self.wide, other_narrow)
        self.along = (self.wide + 2 * (1 - 2 * self.bit), self.narrow)
        self.opposite = (other_core, other_narrow)
        self.moved = self.core + self.narrow == 1

    def ring(self, chips):
        self.chips = ring_size(chips)
        self.group = self.chip // self.chips
        at = lax.rem(self.chip, self.chips)
        odd = lax.rem(at, 2)
        self.place = odd * (self.chips - 1 - at // 2) + (1 - odd) * (at // 2)
        self.right, self.left = self.ring_device(1), self.ring_device(-1)
        self.bits = []
        for bit in range(chips.bit_length() - 1):
            side = lax.rem(self.chip // 2**bit, 2)
            self.bits.append((self.wide + 2 ** (bit + 1) * (1 - 2 * side), self.narrow))
        self.further = self.bits[self.chips.bit_length() - 1 :]

    def ring_device(self, offset):
        place = lax.rem(self.place + offset + self.chips, self.chips)
        late = place // (self.chips // 2)
        chip = late * (2 * (self.chips - 1 - place) + 1) + (1 - late) * (2 * place)
        return (2 * (self.group * self.chips + chip) + self.core, self.narrow)

    def greet(self, devices):
        barrier = pltpu.get_barrier_semaphore()
        for device in devices:
            pl.semaphore_signal(barrier, inc=1, device_id=device, device_id_type=pl.DeviceIdType.MESH)
        pl.semaphore_wait(barrier, len(devices))


def remote(source, target, sems, at, device):
    return pltpu.make_async_remote_copy(
        source, target, sems[0].at[at], sems[1].at[at], device_id=device, device_id_type=pl.DeviceIdType.MESH
    )


class Weight:
    def __init__(self, links, number, own, buffer, local_sem, sems):
        self.links, self.number, self.own, self.buffer, self.local_sem, self.sems = links, number, own, buffer, local_sem, sems
        self.half = buffer.shape[1] // 2

    def rows(self, bit):
        return pl.ds(pl.multiple_of(bit * self.half, 16), self.half)

    def local_copies(self):
        core = self.links.core
        return [
            pltpu.make_async_copy(self.own(core, slice(None)), self.buffer.at[0], self.local_sem.at[2 * self.number]),
            pltpu.make_async_copy(self.own(1 - core, slice(None)), self.buffer.at[2], self.local_sem.at[2 * self.number + 1]),
        ]

    def hop(self, kind):
        links, rows = self.links, self.rows(self.links.bit)
        at = 4 * self.number + kind
        if kind == 0:
            return remote(self.own(links.core, rows), self.buffer.at[1, rows], self.sems, at, links.across)
        if kind == 1:
            return remote(self.buffer.at[1, rows], self.buffer.at[1, rows], self.sems, at, links.along)
        if kind == 3:
            rows = self.rows(1 - links.bit)
        return remote(self.buffer.at[1, rows], self.buffer.at[3, rows], self.sems, at, links.beside)

    def start(self):
        self.hop(0).start()

    def start_local(self):
        for copy in self.local_copies():
            copy.start()

    def relay(self):
        self.hop(0).wait_recv()
        self.hop(1).start()
        self.hop(2).start()

    def relay_again(self):
        self.hop(1).wait_recv()
        self.hop(3).start()

    def wait_own(self):
        for copy in self.local_copies():
            copy.wait()

    def wait_fetched(self):
        self.hop(2).wait_recv()
        self.hop(3).wait_recv()

    def wait_sent(self):
        for kind in range(4):
            self.hop(kind).wait_send()


def ordered(step):
    return lax.rem(2 * step, 4) + step // 2


def at_step(step, hooks):
    for number, hook in enumerate(hooks):
        if hook:

            @pl.when(step == number)
            def _(hook=hook):
                for action in hook:
                    action()


def all_forward(layers, *refs):
    (flag, tokens, cotangent, small, vectors, wi_own, wo_own, we_own, ws_own), refs = refs[:9], refs[9:]
    (rows_ref, cotangent_in, flag_in), refs = refs[:3], refs[3:]
    kept = [refs[STATES * layer : STATES * (layer + 1)] for layer in range(layers)]
    refs = refs[STATES * layers :]
    states = [refs[STATES * layer : STATES * (layer + 1)] for layer in range(layers)]
    refs = refs[STATES * layers :]
    tokens_in = states[0][16]
    (save_sem, small_in, acc, rows_low, rows_in, local_sem, send_sem, recv_sem, kv_send, kv_recv, misc_send, misc_recv) = refs
    links = Links()
    core = links.core
    sems = (send_sem, recv_sem)
    units = ws_own.shape[2]
    width = wo_own.shape[2]
    rows = tokens.shape[0]
    weights = []
    for layer in range(layers):
        buffers = states[layer][:4]
        owns = [
            lambda part, rows, layer=layer: wi_own.at[layer, part, rows],
            lambda part, rows, layer=layer: wo_own.at[layer, part, rows],
            lambda part, rows, layer=layer: we_own.at[layer, rows, pl.ds(pl.multiple_of(part * units, 128), units)],
            lambda part, rows, layer=layer: ws_own.at[layer, part, rows],
        ]
        weights.append([Weight(links, 4 * layer + number, owns[number], buffers[number], local_sem, sems) for number in range(4)])
    every = [weight for group in weights for weight in group]
    for weight in every[:4]:
        weight.start_local()
    links.greet([links.across, links.along, links.beside, links.opposite])
    misc = (misc_send, misc_recv)
    swap_tokens = remote(tokens, tokens_in, misc, 0, links.opposite)
    swap_flag = remote(flag, flag_in, misc, 1, links.opposite)
    copy_small = remote(small, small_in, misc, 2, links.across)
    swap_cotangent = remote(cotangent, cotangent_in, misc, 3, links.opposite)
    swap_rows = remote(rows_low, rows_in, misc, 4, links.opposite)
    copy_small.start()

    @pl.when(links.moved)
    def _():
        swap_tokens.start()
        swap_flag.start()

    @pl.when(jnp.logical_not(links.moved))
    def _():
        tokens_in[...] = tokens[...]
        cotangent_in[...] = cotangent[...]
        flag_in[...] = flag[...]

    for weight in every[:4]:
        weight.start()

    @pl.when(links.moved)
    def _():
        swap_cotangent.start()

    for weight in every[4:]:
        weight.start()
        weight.start_local()

    def bias(layer, at, size, index):
        part = core + (index // 2) * (1 - 2 * core)
        place = pl.ds(pl.multiple_of(at + part * size, 128), size)
        return jnp.where(lax.rem(index, 2) == 0, small[layer : layer + 1, place], small_in[layer : layer + 1, place])

    @pl.when(links.moved)
    def _():
        swap_tokens.wait_recv()
        swap_flag.wait_recv()

    copy_small.wait_recv()
    shift = jnp.where(flag_in[0:1, 0:1] < 0.5, 0.0, MASKED)
    acc[...] = tokens_in[...].astype(F32)
    halves = lane_halves((rows, width))

    def save_copy(layer, number):
        return pltpu.make_async_copy(states[layer][number], kept[layer][number], save_sem.at[layer, number])

    def save(layer, *numbers):
        for number in numbers:
            save_copy(layer, number).start()

    for layer in range(layers):
        (wi, wo, we, ws, query_ref, pair_ref, remote_ref, mixed_ref, total_ref, normed_ref, first_ref, first_scale, active_ref, slope_ref, second_ref, second_scale, low_ref) = states[layer]
        vector = lambda at: vectors[layer, at : at + 1]
        wi_go, wo_go, we_go, ws_go = weights[layer]
        later = weights[layer + 1] if layer + 1 < layers else None
        if layer > 0:
            low_ref[...] = acc[...].astype(BF16)

        def exchange(index):
            return remote(pair_ref.at[index], remote_ref.at[index], (kv_send, kv_recv), (layer, index), links.beside)

        def project(step, carry):
            index = ordered(step)
            triple = dot(low_ref[...], wi[index])
            query = (triple[:, :width] + bias(layer, 0, width, index)).astype(BF16)
            query_ref[index] = query * BF16(DH ** (-0.5))
            pair_ref[index, :, :width] = triple[:, width : 2 * width].astype(BF16)
            pair_ref[index, :, width:] = (triple[:, 2 * width :] + bias(layer, 2 * width, width, index)).astype(BF16)
            exchange(index).start()
            return carry

        if layer == 0:
            before_pair = [
                [wi_go.relay],
                [wo_go.relay, wi_go.relay_again],
                [we_go.relay, wo_go.relay_again, wi_go.wait_fetched, lambda: lax.fori_loop(2, 4, project, 0)],
                [ws_go.relay, we_go.relay_again],
            ]
            before_quarter = [[later[0].relay, ws_go.relay_again], [later[1].relay, later[0].relay_again], [we_go.wait_fetched, ws_go.wait_fetched, later[1].relay_again], [later[2].relay]] if later else [[ws_go.relay_again], [], [we_go.wait_fetched, ws_go.wait_fetched], []]
            wi_go.wait_own()
            lax.fori_loop(0, 2, project, 0)
        else:
            before_pair = [[ws_go.relay, we_go.relay_again], [], [ws_go.relay_again], []]
            before_quarter = [[], [], [we_go.wait_fetched, ws_go.wait_fetched], []]
            wi_go.wait_own()
            wi_go.wait_fetched()
            lax.fori_loop(0, 4, project, 0)
        acc[...] += vector(0)
        wo_go.wait_own()
        before_pair[2].append(wo_go.wait_fetched)

        def one_pair(step, carry):
            at_step(step, before_pair)
            index = ordered(step)
            there = lax.rem(index + 2, 4)
            exchange(there).wait_recv()
            queries = query_ref[index]
            key_here, value_here = pair_ref[index, :, :width], pair_ref[index, :, width:]
            key_there, value_there = remote_ref[there, :, :width], remote_ref[there, :, width:]
            mixed, total = [], []
            for part in range(2):
                mask = halves if part == 0 else jnp.logical_not(halves)
                masked = jnp.where(mask, queries, BF16(0))
                here = dot_rt(masked, key_here)
                away = dot_rt(masked, key_there)
                peak = jnp.maximum(jnp.max(here, -1, keepdims=True), jnp.max(away, -1, keepdims=True) + shift)
                here = jnp.exp(here - peak)
                away = jnp.exp(away - (peak - shift))
                weight = jnp.sum(here, -1, keepdims=True) + jnp.sum(away, -1, keepdims=True)
                both = dot(here.astype(BF16), value_here) + dot(away.astype(BF16), value_there)
                mixed.append(both * (1.0 / weight))
                total.append(jnp.broadcast_to(peak + jnp.log(weight), (rows, width)))
            mixed_low = jnp.where(halves, mixed[0], mixed[1]).astype(BF16)
            mixed_ref[index] = mixed_low
            totals = jnp.where(halves, total[0], total[1]).T
            total_ref[index] = jnp.concatenate([totals[0:8], totals[DH : DH + 8]], 0)
            acc[...] += dot(mixed_low, wo[index])
            return carry

        lax.fori_loop(0, 4, one_pair, 0)
        save(layer, 16, 0, 4, 5, 6, 1, 7, 8)
        first, scale = normalise(acc[...])
        first_ref[...] = first
        first_scale[...] = scale
        normed = first * vector(1) + vector(2)
        normed_ref[...] = normed.astype(BF16)
        acc[...] = normed + vector(3)
        save(layer, 9, 10, 11)
        we_go.wait_own()
        ws_go.wait_own()

        def one_quarter(step, carry):
            at_step(step, before_quarter)
            index = ordered(step)
            active, slope = gelu_parts(dot(normed_ref[...], we[index]) + bias(layer, 4 * width, units, index))
            active_low = active.astype(BF16)
            active_ref[index] = active_low
            slope_ref[index] = slope.astype(BF16)
            acc[...] += dot(active_low, ws[index])
            return carry

        lax.fori_loop(0, 4, one_quarter, 0)
        save(layer, 2, 3, 12, 13)
        second, scale = normalise(acc[...])
        second_ref[...] = second
        second_scale[...] = scale
        save(layer, 14, 15)
        acc[...] = second * vector(4) + vector(5)

    rows_low[...] = acc[...].astype(BF16)

    @pl.when(links.moved)
    def _():
        swap_rows.start()
        swap_rows.wait_recv()
        rows_ref[...] = rows_in[...].astype(F32)

    @pl.when(jnp.logical_not(links.moved))
    def _():
        rows_ref[...] = acc[...]

    @pl.when(links.moved)
    def _():
        swap_cotangent.wait_recv()
        for copy in (swap_tokens, swap_flag, swap_cotangent, swap_rows):
            copy.wait_send()

    copy_small.wait_send()
    for weight in every:
        weight.wait_sent()
    for layer in range(layers):
        for number in range(STATES):
            save_copy(layer, number).wait()
    for layer in range(layers):
        pair_ref, remote_ref = states[layer][5:7]
        for index in range(4):
            remote(pair_ref.at[index], remote_ref.at[index], (kv_send, kv_recv), (layer, index), links.beside).wait_send()


def column_sum(x):
    return jnp.sum(x, 0, keepdims=True)


def norm_backward(grad, normed, scale, gain):
    scaled = grad * gain
    return (
        scaled - jnp.mean(scaled, -1, keepdims=True) - normed * jnp.mean(scaled * normed, -1, keepdims=True)
    ) * scale


def backwards(step):
    return 3 - ordered(step)


class Gradient:
    def __init__(self, links, number, mine, theirs, core_in, narrow_in, slots, further_in, out, columns, sems):
        self.links, self.number, self.mine, self.theirs, self.core_in = links, number, mine, theirs, core_in
        self.narrow_in, self.slots, self.further_in, self.out, self.columns, self.sems = narrow_in, slots, further_in, out, columns, sems
        self.size = core_in.shape[1]
        self.piece = mine.shape[1] // links.chips

    def part_copy(self, part):
        return remote(self.theirs.at[part], self.core_in.at[part], self.sems[0], (self.number, part), self.links.beside)

    def narrow_copy(self):
        return remote(self.mine.at[1, pl.ds(0, self.size)], self.narrow_in, self.sems[0], (self.number, 2), self.links.across)

    def share_copy(self):
        place = self.out.at[self.links.core]
        return remote(place, place, self.sems[0], (self.number, 3), self.links.beside)

    def ring_copy(self, side, step):
        links, way = self.links, 1 - 2 * side
        at, count = self.columns[side]
        device = links.right if side == 0 else links.left
        where = (self.number, side, step)
        if step < links.chips - 1:
            source = self.mine.at[0, self.rows(-way * step), pl.ds(at, count)]
            return remote(source, self.slots[side].at[step], self.sems[1], where, device)
        rows = self.rows(-way * (step - links.chips))
        target = self.out.at[links.core, rows, pl.ds(at, count)]
        source = self.mine.at[0, rows, pl.ds(at, count)] if step == links.chips - 1 else target
        return remote(source, target, self.sems[1], where, device)

    def further_copy(self, side, number):
        at, count = self.columns[side]
        source = self.mine.at[0, self.rows(1 - 2 * side), pl.ds(at, count)]
        return remote(source, self.further_in[side].at[number], self.sems[2], (self.number, side, number), self.links.further[number])

    def rows(self, offset):
        index = lax.rem(self.links.place + offset + 2 * self.links.chips, self.links.chips)
        return pl.ds(pl.multiple_of(index * self.piece, 16), self.piece)

    def send(self, part):
        self.part_copy(part).start()

    def middle(self):
        self.part_copy(1).wait_recv()
        total = self.mine[1, 0 : self.size].astype(F32) + self.core_in[1].astype(F32)
        self.mine[1, 0 : self.size] = total.astype(BF16)
        self.narrow_copy().start()

    def settle(self):
        self.part_copy(0).wait_recv()
        self.narrow_copy().wait_recv()
        total = self.mine[0, 0 : self.size].astype(F32) + self.core_in[0].astype(F32) + self.narrow_in[...].astype(F32)
        self.mine[0, 0 : self.size] = total.astype(BF16)
        for side in range(2):
            self.ring_copy(side, 0).start()

    def tick(self, step):
        chips = self.links.chips
        for side in range(2):
            way = 1 - 2 * side
            at, count = self.columns[side]
            self.ring_copy(side, step).wait_recv()
            if step < chips - 1:
                rows = self.rows(-way * (step + 1))
                total = self.mine[0, rows, at : at + count].astype(F32) + self.slots[side][step].astype(F32)
                total = total.astype(BF16)
                self.mine[0, rows, at : at + count] = total
                for number in range(len(self.links.further) if step == chips - 2 else 0):
                    copy = self.further_copy(side, number)
                    copy.start()
                    copy.wait()
                    total = (total.astype(F32) + self.further_in[side][number].astype(F32)).astype(BF16)
                    self.mine[0, rows, at : at + count] = total
                if step == chips - 2:
                    self.out[self.links.core, rows, at : at + count] = total
            if step < 2 * chips - 3:
                self.ring_copy(side, step + 1).start()

    def share(self):
        self.share_copy().start()

    def free_theirs(self):
        for part in range(2):
            self.part_copy(part).wait_send()

    def wait_all(self, theirs_waited):
        self.share_copy().wait_recv()
        self.share_copy().wait_send()
        if not theirs_waited:
            self.free_theirs()
        self.narrow_copy().wait_send()
        for side in range(2):
            for step in range(2 * self.links.chips - 2):
                self.ring_copy(side, step).wait_send()


def all_backward(layers, chips, *refs):
    (flag, vectors, cotangent), refs = refs[:3], refs[3:]
    kept = [refs[STATES * layer : STATES * (layer + 1)] for layer in range(layers)]
    refs = refs[STATES * layers :]
    (rows_ref, small_out), refs = refs[:2], refs[2:]
    outs = [refs[3 * layer : 3 * layer + 3] for layer in range(layers)]
    refs = refs[3 * layers :]
    state, refs = refs[:STATES], refs[STATES:]
    (acc, turned, summed_ref, mixed_grad_ref, inner_ref, query_grad_ref, here_ref, away_ref, rows_low, rows_in), refs = refs[:10], refs[10:]
    away_in, refs = refs[:layers], refs[layers:]
    theirs, refs = refs[:3], refs[3:]
    buffers = [refs[21 * layer : 21 * layer + 21] for layer in range(layers)]
    refs = refs[21 * layers :]
    (small, core_small, mid_small, row_small, sum_small, step_small), refs = refs[:6], refs[6:]
    (load_sem, away_send, away_recv, grad_send, grad_recv, ring_send, ring_recv, misc_send, misc_recv, step_send, step_recv, further_send, further_recv) = refs
    (wi, wo, we, ws, query, pair, remote_pair, mixed, total_ref, normed, first, first_scale, active, slope, second, second_scale, hidden_low) = state
    links = Links()
    links.ring(chips)
    core = links.core
    steps = chips.bit_length() - 1
    bits = links.bits

    def load_copy(layer, number):
        return pltpu.make_async_copy(kept[layer][number], state[number], load_sem.at[number])

    def load(layer, numbers):
        for number in numbers:
            load_copy(layer, number).start()

    def loaded(layer, *numbers):
        for number in numbers:
            load_copy(layer, number).wait()

    block_group = (14, 15, 3, 13, 12, 2, 9, 10, 11, 1, 7)
    pair_group = (4, 5, 6, 8)
    input_group = (16, 0)
    load(layers - 1, block_group + pair_group + input_group)
    links.greet([links.across, links.beside, links.opposite, links.right, links.left] + bits)
    misc = (misc_send, misc_recv)
    gradients = []
    for layer in range(layers):
        group = []
        for kind in range(3):
            mine, core_in, narrow_in, slot_one, slot_two, further_one, further_two = buffers[layer][7 * kind : 7 * kind + 7]
            if kind < 2:
                half = mine.shape[2] // 2
                columns = ((0, half), (half, half))
            else:
                third = mine.shape[2] // 3
                columns = ((0, 2 * third), (2 * third, third))
            group.append(Gradient(
                links, 3 * layer + kind, mine, theirs[kind], core_in, narrow_in, (slot_one, slot_two), (further_one, further_two), outs[layer][kind], columns,
                ((grad_send, grad_recv), (ring_send, ring_recv), (further_send, further_recv)),
            ))
        gradients.append(group)
    rows, width = mixed.shape[1], mixed.shape[2]
    units, depth = ws.shape[1], ws.shape[2]
    halves = lane_halves((rows, width))
    shift = jnp.where(flag[0:1, 0:1] < 0.5, 0.0, MASKED)
    small[...] = jnp.zeros(small.shape, F32)
    half = lax.broadcasted_iota(jnp.int32, (16, width), 1) // DH
    which = lax.broadcasted_iota(jnp.int32, (16, width), 0) // 8
    selector = (half == which).astype(F32)
    acc[...] = cotangent[...].astype(F32)
    for layer in reversed(range(layers)):
        feed, output, inputs = gradients[layer]
        before = gradients[layer + 1] if layer + 1 < layers else None
        vector = lambda at: vectors[layer, at : at + 1]

        def put(gradient, index, at, value):
            @pl.when(index < 2)
            def _():
                gradient.mine[index, at : at + value.shape[0]] = value

            @pl.when(index >= 2)
            def _():
                gradient.theirs[index - 2, at : at + value.shape[0]] = value

        def tick(kind, step):
            return lambda: before[kind].tick(step)

        loaded(layer, 14, 15)
        incoming = acc[...]
        widened = norm_backward(incoming, second[...], second_scale[...], vector(4))
        sums = [column_sum(incoming), column_sum(incoming * second[...]), column_sum(widened)]
        acc[...] = widened
        rows_low[...] = widened.astype(BF16)
        loaded(layer, 9)
        turned[...] = normed[...].T
        loaded(layer, 3, 13, 12, 2)
        if before:
            for gradient in before:
                gradient.free_theirs()
        block_hooks = [[], [functools.partial(feed.send, 1)], [feed.middle], [functools.partial(feed.send, 0)]]
        if before:
            block_hooks[0].append(before[0].settle)
            for number in range(3):
                block_hooks[number + 1].append(tick(0, number))

        def one_quarter(step, carry):
            at_step(step, block_hooks)
            index = backwards(step)
            branch = rows_low[...]
            inner = (dot_rt(branch, ws[index]) * slope[index].astype(F32)).astype(BF16)
            put(feed, index, 0, dot_lt(active[index], branch).astype(BF16))
            put(feed, index, units, dot(turned[...], inner).astype(BF16))
            small[index, 8 * layer + 6 : 8 * layer + 7, 0:units] = column_sum(inner.astype(F32))
            acc[...] += dot_rt(inner, we[index])
            return carry

        lax.fori_loop(0, 4, one_quarter, 0)
        loaded(layer, 10, 11, 1, 7)
        outgoing = acc[...]
        summed = norm_backward(outgoing, first[...], first_scale[...], vector(1))
        sums += [column_sum(outgoing), column_sum(outgoing * first[...]), column_sum(summed)]
        for number, value in enumerate(sums):
            for quarter in range(4):
                small[quarter, 8 * layer + number : 8 * layer + number + 1] = value
        summed_ref[...] = summed
        rows_low[...] = summed.astype(BF16)
        if before:
            before[0].tick(3)
            before[1].settle()

        def one_output(step, carry):
            index = backwards(step)
            mixed_grad = dot_rt(rows_low[...], wo[index]).astype(BF16)
            mixed_grad_ref[index] = mixed_grad
            put(output, index, 0, dot_lt(mixed[index], rows_low[...]).astype(BF16))
            product = mixed_grad.astype(F32) * mixed[index].astype(F32)
            inner_ref[index] = lax.dot_general(
                selector, product, (((1,), (1,)), ((), ())), precision=lax.Precision.HIGHEST, preferred_element_type=F32
            )
            return carry

        lax.fori_loop(0, 4, one_output, 0)
        output.send(0)
        output.send(1)
        if layer > 0:
            load(layer - 1, block_group)
        loaded(layer, *pair_group)
        pair_hooks = [[], [output.middle], [], []]
        if before:
            pair_hooks[0] += [tick(0, 4), before[2].settle]
            pair_hooks[1] += [tick(0, 5), tick(1, 0), tick(2, 0)]
            pair_hooks[2] += [tick(0, 6), tick(1, 1), tick(2, 1)]
            pair_hooks[3] += [tick(0, 7), tick(1, 2), tick(2, 2)]

        def away_copy(there):
            return remote(away_ref.at[there], away_in[layer].at[there], (away_send, away_recv), (layer, there), links.beside)

        if before:
            for there in range(4):
                remote(away_ref.at[there], away_in[layer + 1].at[there], (away_send, away_recv), (layer + 1, there), links.beside).wait_send()

        def one_pair(step, carry):
            at_step(step, pair_hooks)
            there = backwards(step)
            index = lax.rem(there + 2, 4)
            queries, grads = query[index], mixed_grad_ref[index]
            query_turned = None
            for side in range(2):
                source, place = (pair, index) if side == 0 else (remote_pair, there)
                keys, values = source[place, :, :width], source[place, :, width:]
                key_grad = value_grad = None
                for part in range(2):
                    mask = halves if part == 0 else jnp.logical_not(halves)
                    masked_query = jnp.where(mask, queries, BF16(0))
                    masked_grad = jnp.where(mask, grads, BF16(0))
                    masked_key = jnp.where(mask, keys, BF16(0))
                    level = total_ref[index, 8 * part : 8 * part + 1]
                    if side == 1:
                        level = level - shift
                    weights = jnp.exp(dot_rt(keys, masked_query) - level)
                    update = dot(weights.astype(BF16), masked_grad)
                    value_grad = update if value_grad is None else value_grad + update
                    slopes = dot_rt(values, masked_grad) - inner_ref[index, 8 * part : 8 * part + 1]
                    slopes = (weights * slopes).astype(BF16)
                    update = dot(slopes, masked_query)
                    key_grad = update if key_grad is None else key_grad + update
                    update = dot_lt(masked_key, slopes)
                    query_turned = update if query_turned is None else query_turned + update
                if side == 0:
                    here_ref[index, :, :width] = key_grad
                    here_ref[index, :, width:] = value_grad
                else:
                    away_ref[there, :, :width] = key_grad.astype(BF16)
                    away_ref[there, :, width:] = value_grad.astype(BF16)
            away_copy(there).start()
            query_grad_ref[index] = (query_turned * DH ** (-0.5)).T.astype(BF16)
            return carry

        lax.fori_loop(0, 4, one_pair, 0)
        if layer > 0:
            load(layer - 1, pair_group)
        loaded(layer, *input_group)
        turned[...] = hidden_low[...].T
        acc[...] = summed_ref[...]
        input_hooks = [[], [functools.partial(inputs.send, 1)], [inputs.middle], [functools.partial(inputs.send, 0)]]
        if before:
            input_hooks[0] += [tick(0, 8)]
            input_hooks[1] += [tick(1, 3), tick(2, 3)]
            input_hooks[2] += [tick(0, 9)]
            input_hooks[3] += [tick(1, 4), tick(2, 4)]

        def one_input(step, carry):
            at_step(step, input_hooks)
            index = backwards(step)
            away_copy(index).wait_recv()
            pair_grad = (here_ref[index] + away_in[layer][index].astype(F32)).astype(BF16)
            triple = jnp.concatenate([query_grad_ref[index], pair_grad], 1)
            put(inputs, index, 0, dot(turned[...], triple).astype(BF16))
            acc[...] += dot_rt(triple, wi[index])
            small[index, 8 * layer + 7 : 8 * layer + 8, 0 : 3 * width] = column_sum(triple.astype(F32))
            return carry

        lax.fori_loop(0, 4, one_input, 0)
        if layer > 0:
            load(layer - 1, input_group)

    feed, output, inputs = gradients[0]
    rows_low[...] = acc[...].astype(BF16)
    swap_rows = remote(rows_low, rows_in, misc, 0, links.opposite)
    copy_core = remote(small.at[pl.ds(2, 2)], core_small, misc, 1, links.beside)
    copy_row = remote(mid_small, row_small, misc, 2, links.across)
    share_small = remote(small_out.at[core], small_out.at[core], misc, 3, links.beside)

    def step_copy(step):
        return remote(sum_small.at[step], step_small.at[step], (step_send, step_recv), step, bits[step])

    copy_core.start()

    @pl.when(links.moved)
    def _():
        swap_rows.start()

    copy_core.wait_recv()
    mid_small[...] = small[1] + core_small[1]
    copy_row.start()
    ticks = 2 * links.chips - 2
    queues = []
    if layers > 1:
        queues += [(0, gradients[1][0], 10), (0, gradients[1][1], 5), (0, gradients[1][2], 5)]
    feed_at, late_at = 0, 3
    queues += [(feed_at + 1, feed, 0), (late_at + 1, output, 0), (late_at + 1, inputs, 0)]
    for gradient in gradients[2:]:
        pass
    value = None
    for step in range(late_at + 1 + ticks):
        if step == feed_at:
            feed.settle()
        if step == late_at:
            output.settle()
            inputs.settle()
        for start, gradient, done in queues:
            at = step - start + done
            if step >= start and at < ticks:
                gradient.tick(at)
                if at == ticks - 1:
                    gradient.share()
        if step == 1:
            copy_row.wait_recv()
            value = small[0] + core_small[0] + row_small[...]
        if 1 < step <= steps + 1:
            step_copy(step - 2).wait_recv()
            value = value + step_small[step - 2]
        if 1 <= step <= steps:
            sum_small[step - 1] = value
            step_copy(step - 1).start()
        if step == steps + 1:
            small_out[core] = value
            share_small.start()

    @pl.when(links.moved)
    def _():
        swap_rows.wait_recv()
        swap_rows.wait_send()
        rows_ref[...] = rows_in[...].astype(F32)

    @pl.when(jnp.logical_not(links.moved))
    def _():
        rows_ref[...] = acc[...]

    share_small.wait_recv()
    share_small.wait_send()
    copy_core.wait_send()
    copy_row.wait_send()
    for step in range(steps):
        step_copy(step).wait_send()
    for there in range(4):
        remote(away_ref.at[there], away_in[0].at[there], (away_send, away_recv), (0, there), links.beside).wait_send()
    for layer in range(layers):
        for gradient in gradients[layer]:
            gradient.wait_all(layer > 0)


def assemble_kernel(layers, *refs):
    ins, refs = refs[: 3 * layers], refs[3 * layers :]
    (shrink_ref, expand_ref, output_ref, input_ref) = refs
    for layer in range(layers):
        feed, output, inputs = ins[3 * layer : 3 * layer + 3]
        units, depth = expand_ref.shape[2] // 2, expand_ref.shape[1]
        width = output_ref.shape[1] // 2
        for part in range(2):
            shrink_ref[layer, part * units : (part + 1) * units] = feed[part, 0:units].astype(F32)
            expand_ref[layer, :, part * units : (part + 1) * units] = feed[part, units : units + depth].astype(F32)
            output_ref[layer, part * width : (part + 1) * width] = output[part, 0:width].astype(F32)
            for kind in range(3):
                input_ref[kind, layer, :, part * width : (part + 1) * width] = inputs[part, 0:depth, kind * width : (kind + 1) * width].astype(F32)


VM = pl.BlockSpec(memory_space=pltpu.VMEM)
AN = pl.BlockSpec(memory_space=pl.ANY)


def shaped(dtype, *dims):
    return jax.ShapeDtypeStruct(dims, dtype)


def cost(flops, size):
    return pl.CostEstimate(flops=flops, bytes_accessed=size, transcendentals=0)


def local(
    tokens, input_weight, query_bias, value_bias, output_weight, output_bias, first_gain, first_shift,
    expand_weight, expand_bias, shrink_weight, shrink_bias, second_gain, second_shift, lengths, bucket, cotangent,
):
    wide, narrow = lax.axis_size("wide"), lax.axis_size("narrow")
    assert narrow == 2 and wide % 2 == 0
    layers, depth = input_weight.shape[0], input_weight.shape[1]
    rows = tokens.shape[0]
    width = input_weight.shape[3] // 2
    units = expand_weight.shape[2] // 2

    flag = jnp.broadcast_to(bucket, (8, 128)).astype(F32)
    input_own = (
        input_weight.reshape(layers, depth, 3, 2, width).transpose(0, 3, 1, 2, 4).reshape(layers, 2, depth, 3 * width)
    )
    output_own = output_weight.reshape(layers, 2, width, depth)
    shrink_own = shrink_weight.reshape(layers, 2, units, depth)
    small = jnp.concatenate([query_bias, value_bias, expand_bias], 1)
    vectors = jnp.stack(
        [output_bias, first_gain, first_shift, shrink_bias, second_gain, second_shift, output_bias, output_bias], 1
    )
    query_shape = shaped(BF16, 4, rows, width)
    pair_shape = shaped(BF16, 4, rows, 2 * width)
    row_shape = shaped(F32, rows, depth)
    low_shape = shaped(BF16, rows, depth)
    scale_shape = shaped(F32, rows, 1)
    stat_shape = shaped(F32, 4, 16, rows)
    wide_shape = shaped(BF16, 4, rows, units)
    state_shapes = [
        shaped(BF16, 4, depth, 3 * width), shaped(BF16, 4, width, depth), shaped(BF16, 4, depth, units), shaped(BF16, 4, units, depth),
        query_shape, pair_shape, pair_shape, query_shape, stat_shape, low_shape, row_shape, scale_shape, wide_shape, wide_shape, row_shape, scale_shape, low_shape,
    ]
    state_scratch = [pltpu.VMEM(shape.shape, shape.dtype) for shape in state_shapes]
    kept_shapes = state_shapes * layers
    results = pl.pallas_call(
        functools.partial(all_forward, layers),
        out_shape=[row_shape, low_shape, shaped(F32, 8, 128)] + kept_shapes,
        in_specs=[VM] * 5 + [AN] * 4,
        out_specs=[VM] * 3 + [AN] * len(kept_shapes),
        scratch_shapes=state_scratch * layers + [
            pltpu.SemaphoreType.DMA((layers, STATES)),
            pltpu.VMEM(small.shape, F32), pltpu.VMEM((rows, depth), F32), pltpu.VMEM((rows, depth), BF16), pltpu.VMEM((rows, depth), BF16),
            pltpu.SemaphoreType.DMA((8 * layers,)),
            pltpu.SemaphoreType.DMA((16 * layers,)), pltpu.SemaphoreType.DMA((16 * layers,)),
            pltpu.SemaphoreType.DMA((layers, 4)), pltpu.SemaphoreType.DMA((layers, 4)),
            pltpu.SemaphoreType.DMA((5,)), pltpu.SemaphoreType.DMA((5,)),
        ],
        compiler_params=pltpu.CompilerParams(collective_id=1, has_side_effects=True, vmem_limit_bytes=62 * 2**20),
        cost_estimate=cost(10**10, 10**8),
        name="forward",
    )(flag, tokens, cotangent, small, vectors, input_own, output_own, expand_weight, shrink_own)
    layer_output, cotangent, flag = results[:3]
    chips = wide // 2
    ring = ring_size(chips)
    further = (chips // ring).bit_length() - 1
    tall = lambda size: -(-size // (16 * ring)) * 16 * ring
    out_shapes, buffer_scratch, theirs_scratch = [], [], []
    for size, columns, first_columns in ((units + depth, depth, depth // 2), (width, depth, depth // 2), (depth, 3 * width, 2 * width)):
        out_shapes.append(shaped(BF16, 2, tall(size), columns))
        theirs_scratch.append(pltpu.VMEM((2, size, columns), BF16))
        slot = lambda count: pltpu.VMEM((ring - 1, tall(size) // ring, count), BF16)
        more = lambda count: pltpu.VMEM((further, tall(size) // ring, count) if further else (1, 16, 128), BF16)
        buffer_scratch += [
            pltpu.VMEM((2, tall(size), columns), BF16), pltpu.VMEM((2, size, columns), BF16), pltpu.VMEM((size, columns), BF16),
            slot(first_columns), slot(columns - first_columns), more(first_columns), more(columns - first_columns),
        ]
    small_rows = 8 * layers
    steps = chips.bit_length() - 1
    small_scratch = pltpu.VMEM((small_rows, depth), F32)
    ring_sem = pltpu.SemaphoreType.DMA((3 * layers, 2, 2 * ring - 2))
    further_sem = pltpu.SemaphoreType.DMA((3 * layers, 2, max(further, 1)))
    results = pl.pallas_call(
        functools.partial(all_backward, layers, chips),
        out_shape=[row_shape, shaped(F32, 2, small_rows, depth)] + out_shapes * layers,
        in_specs=[VM] * 3 + [AN] * len(kept_shapes),
        out_specs=[VM] * (2 + 3 * layers),
        scratch_shapes=state_scratch + [
            pltpu.VMEM((rows, depth), F32), pltpu.VMEM((depth, rows), BF16), pltpu.VMEM((rows, depth), F32),
            pltpu.VMEM(query_shape.shape, BF16), pltpu.VMEM(stat_shape.shape, F32), pltpu.VMEM(query_shape.shape, BF16),
            pltpu.VMEM(pair_shape.shape, F32), pltpu.VMEM(pair_shape.shape, BF16), pltpu.VMEM((rows, depth), BF16), pltpu.VMEM((rows, depth), BF16),
        ] + [pltpu.VMEM(pair_shape.shape, BF16)] * layers + theirs_scratch + buffer_scratch * layers + [
            pltpu.VMEM((4, small_rows, depth), F32), pltpu.VMEM((2, small_rows, depth), F32), small_scratch, small_scratch,
            pltpu.VMEM((steps, small_rows, depth), F32), pltpu.VMEM((steps, small_rows, depth), F32),
            pltpu.SemaphoreType.DMA((STATES,)),
            pltpu.SemaphoreType.DMA((layers, 4)), pltpu.SemaphoreType.DMA((layers, 4)),
            pltpu.SemaphoreType.DMA((3 * layers, 4)), pltpu.SemaphoreType.DMA((3 * layers, 4)),
            ring_sem, ring_sem,
            pltpu.SemaphoreType.DMA((4,)), pltpu.SemaphoreType.DMA((4,)),
            pltpu.SemaphoreType.DMA((steps,)), pltpu.SemaphoreType.DMA((steps,)), further_sem, further_sem,
        ],
        compiler_params=pltpu.CompilerParams(collective_id=0, has_side_effects=True, vmem_limit_bytes=67043328),
        cost_estimate=cost(10**10, 10**8),
        name="backward",
    )(flag, vectors, cotangent, *results[3:])
    input_rows, small = results[:2]
    shrink_grad, expand_grad, output_grad, input_grad = pl.pallas_call(
        functools.partial(assemble_kernel, layers),
        out_shape=[
            shaped(F32, layers, 2 * units, depth), shaped(F32, layers, depth, 2 * units), shaped(F32, layers, 2 * width, depth),
            shaped(F32, 3, layers, depth, 2 * width),
        ],
        in_specs=[VM] * (3 * layers),
        out_specs=[VM] * 4,
        compiler_params=pltpu.CompilerParams(vmem_limit_bytes=40 * 2**20),
        cost_estimate=cost(10**6, 2 * 10**7),
        name="assemble",
    )(*results[2:])
    small = small.reshape(2, layers, 8, depth)
    both = lambda at, a, b: small[:, :, at, a:b].transpose(1, 0, 2).reshape(layers, 2 * (b - a))
    vector = lambda at: small[0, :, at]
    return (
        layer_output,
        input_rows,
        input_grad.transpose(1, 2, 0, 3),
        both(7, 0, width),
        both(7, 2 * width, 3 * width),
        output_grad,
        vector(5),
        vector(4),
        vector(3),
        expand_grad,
        both(6, 0, units),
        shrink_grad,
        vector(2),
        vector(1),
        vector(0),
    )


def solution(mesh):
    split = P(AXES, None)
    in_specs = (
        split, P(None, None, None, "narrow"), P(None, "narrow"), P(None, "narrow"), P(None, "narrow", None), P(), P(), P(),
        P(None, None, "narrow"), P(None, "narrow"), P(None, "narrow", None), P(), P(), P(), P("wide"), P("wide"), split,
    )
    out_specs = (
        split, split, P(None, None, None, "narrow"), P(None, "narrow"), P(None, "narrow"), P(None, "narrow", None), P(), P(), P(),
        P(None, None, "narrow"), P(None, "narrow"), P(None, "narrow", None), P(), P(), P(),
    )
    return jax.shard_map(local, mesh=mesh, in_specs=in_specs, out_specs=out_specs, check_vma=False)
```

profile of v0, /device:TPU:0, one launch (start us, length us, event | category | flops | bytes accessed | tf_op | source)
XLA Modules:
  0.0 269.3 jit_solution(10296319062508667558)
XLA Ops:
  1.3 0.6 broadcast_in_dim.2.refs_0_
  1.9 0.7 stack.23
  2.6 0.7 stack.24
  3.3 0.7 stack.25
  4.0 0.7 stack.26
  4.6 0.7 stack.27
  5.3 0.7 stack.28
  6.0 0.7 stack.29.refs_4_.refs_1_
  6.7 1.3 pad_maximum_fusion.refs_3_
  8.0 1.7 copy.53
  9.7 0.1 copy.54
  9.8 1.6 copy.55.refs_5_
  11.4 81.3 %forward.1 = (f32[512,512]{1,0:T(8,128)}, bf16[512,512]{1,0:T(8,128)(2,1)}, f32[8,128]{1,0:T(8,128)}, bf16[4,512,384]{2,1,0:T(8,128)(2,1)}, bf16[4,128,512]{2,1,...) custom-call(f32[8,128]{1,0:T(8,128)} %broadcast_in_dim.2.refs_0_, ...), custom_call_target="tpu_custom_call" | custom-call | flops 10000000000 | bytes 100000000 | tf_op jit(solution)/shard_map/forward/pallas_call | solution.py:851
  92.7 154.9 %backward.1 = (f32[512,512]{1,0:T(8,128)}, f32[2,16,512]{2,1,0:T(8,128)}, bf16[2,1024,512]{2,1,0:T(8,128)(2,1)}, bf16[2,128,512]{2,1,0:T(8,128)(2,1)}, bf16[2,51...) custom-call(f32[8,128]{1,0:T(8,128)} %get-tuple-element.65.refs_0_, ...), custom_call_target="tpu_custom_call" | custom-call | flops 10000000000 | bytes 100000000 | tf_op jit(solution)/shard_map/backward/pallas_call | solution.py:888
  247.6 1.3 fusion.1
  249.0 0.8 slice.41
  249.8 1.0 fusion
  250.8 0.6 copy.66
  251.4 0.6 copy_bitcast_fusion
  252.0 0.6 copy_bitcast_fusion.2
  252.6 0.6 copy_bitcast_fusion.4
  253.2 1.6 copy-done
  254.8 1.6 copy-done.1
  256.4 1.1 copy-done.2
  257.5 1.1 copy-done.3
  258.7 0.9 copy-done.4
  259.6 0.9 copy-done.5
  260.6 4.1 %assemble.1 = (f32[2,1024,512]{2,1,0:T(8,128)}, f32[2,512,1024]{2,1,0:T(8,128)}, f32[2,256,512]{2,1,0:T(8,128)}, f32[3,2,512,256]{3,2,1,0:T(8,128)S(1)}) custom-call(bf16[2,1024,512]{2,1,0:T(8,128)(2,1)S(1)} %copy-done, bf16[2,128,512]{2,1,0:T(8,128)(2,1)S(1)} %copy-done.4, bf16[2,512,384]{2,1,0:T(8,128)(2,1)S(1)} %copy-done.2, ...), custom_call_target="tpu_custom_call" | custom-call | flops 1000000 | bytes 20000000 | tf_op jit(solution)/shard_map/assemble/pallas_call | solution.py:912
  264.7 2.1 copy.65
  266.7 1.0 copy.82
  267.7 0.6 copy-done.7
  268.3 1.0 copy.83
  (9 shorter events, 0.0 us)
Async XLA Ops:
  253.2 1.6 copy-start
  254.8 1.6 copy-start.1
  256.4 1.1 copy-start.2
  257.5 1.1 copy-start.3
  258.7 0.9 copy-start.4
  259.6 0.9 copy-start.5
  264.7 2.1 copy-start.6
  266.7 1.6 copy-start.7
where the time goes:
time: 270 us; the launch traced here: 269 us
  Pallas kernels  240 us (89%)
  local copies, waits for them, and re-layouts  26.3 us (10%)
    pallas_call x1, Pallas kernels, local(): pl.pallas_call(functools.partial(all_backward, layers, chips), out_shape=...  155 us
    pallas_call x1, Pallas kernels, local(): pl.pallas_call(functools.partial(all_forward, layers), out_shape=[row_sha...  81.3 us
    unnamed x21, local copies, waits for them, and re-layouts  14.3 us

commit v1 on v0

--- a/solution.py
+++ b/solution.py
@@ -65,7 +65,9 @@
         other_core, other_narrow = self.wide + 1 - 2 * self.core, 1 - self.narrow
         self.beside = (other_core, self.narrow)
         self.across = (self.wide, other_narrow)
+        self.next_bit = lax.rem(self.chip // 2, 2)
         self.along = (self.wide + 2 * (1 - 2 * self.bit), self.narrow)
+        self.along_next = (self.wide + 4 * (1 - 2 * self.next_bit), self.narrow)
         self.opposite = (other_core, other_narrow)
         self.moved = self.core + self.narrow == 1
 
@@ -102,58 +104,85 @@
 
 
 class Weight:
-    def __init__(self, links, number, own, buffer, local_sem, sems):
-        self.links, self.number, self.own, self.buffer, self.local_sem, self.sems = links, number, own, buffer, local_sem, sems
-        self.half = buffer.shape[1] // 2
-
-    def rows(self, bit):
-        return pl.ds(pl.multiple_of(bit * self.half, 16), self.half)
+    def __init__(self, links, number, own, parts, buffer, local_sem, sems):
+        self.links, self.number, self.own, self.parts = links, number, own, parts
+        self.buffer, self.local_sem, self.sems = buffer, local_sem, sems
+        self.size = buffer.shape[1] // 4
+        self.columns = buffer.shape[2] // parts
+
+    def rows(self, flip, flip_next):
+        bit = self.links.bit + flip * (1 - 2 * self.links.bit)
+        next_bit = self.links.next_bit + flip_next * (1 - 2 * self.links.next_bit)
+        return pl.ds(pl.multiple_of((2 * next_bit + bit) * self.size, 16), self.size)
 
     def local_copies(self):
         core = self.links.core
+        copies = []
+        for slot, part in ((0, core), (2, 1 - core)):
+            for kind in range(self.parts):
+                target = self.buffer.at[slot, :, pl.ds(kind * self.columns, self.columns)]
+                copies.append(pltpu.make_async_copy(self.own(part, slice(None), kind), target, self.local_sem.at[self.number, len(copies)]))
+        return copies
+
+    def first_hops(self):
+        rows = self.rows(0, 0)
         return [
-            pltpu.make_async_copy(self.own(core, slice(None)), self.buffer.at[0], self.local_sem.at[2 * self.number]),
-            pltpu.make_async_copy(self.own(1 - core, slice(None)), self.buffer.at[2], self.local_sem.at[2 * self.number + 1]),
+            remote(
+                self.own(self.links.core, rows, kind), self.buffer.at[1, rows, pl.ds(kind * self.columns, self.columns)],
+                self.sems, (self.number, kind), self.links.across,
+            )
+            for kind in range(self.parts)
         ]
 
     def hop(self, kind):
-        links, rows = self.links, self.rows(self.links.bit)
-        at = 4 * self.number + kind
-        if kind == 0:
-            return remote(self.own(links.core, rows), self.buffer.at[1, rows], self.sems, at, links.across)
-        if kind == 1:
-            return remote(self.buffer.at[1, rows], self.buffer.at[1, rows], self.sems, at, links.along)
-        if kind == 3:
-            rows = self.rows(1 - links.bit)
+        links = self.links
+        at = (self.number, 2 + kind)
+        device = links.along if kind == 1 or (kind == 3 and self.number % 2) else links.along_next
+        if kind < 3:
+            rows = self.rows(0, 0)
+        elif kind == 3:
+            rows = self.rows(0, 1) if self.number % 2 else self.rows(1, 0)
+        else:
+            rows = self.rows(kind % 2, (kind - 4) // 2)
+        if kind < 4:
+            return remote(self.buffer.at[1, rows], self.buffer.at[1, rows], self.sems, at, device)
         return remote(self.buffer.at[1, rows], self.buffer.at[3, rows], self.sems, at, links.beside)
 
     def start(self):
-        self.hop(0).start()
+        for copy in self.first_hops():
+            copy.start()
 
     def start_local(self):
         for copy in self.local_copies():
             copy.start()
 
     def relay(self):
-        self.hop(0).wait_recv()
-        self.hop(1).start()
-        self.hop(2).start()
+        for copy in self.first_hops():
+            copy.wait_recv()
+        for kind in (1, 2, 4):
+            self.hop(kind).start()
 
     def relay_again(self):
         self.hop(1).wait_recv()
-        self.hop(3).start()
+        self.hop(2).wait_recv()
+        for kind in (3, 5, 6):
+            self.hop(kind).start()
+
+    def relay_last(self):
+        self.hop(3).wait_recv()
+        self.hop(7).start()
 
     def wait_own(self):
         for copy in self.local_copies():
             copy.wait()
 
     def wait_fetched(self):
-        self.hop(2).wait_recv()
-        self.hop(3).wait_recv()
+        for kind in range(4, 8):
+            self.hop(kind).wait_recv()
 
     def wait_sent(self):
-        for kind in range(4):
-            self.hop(kind).wait_send()
+        for copy in self.first_hops() + [self.hop(kind) for kind in range(1, 8)]:
+            copy.wait_send()
 
 
 def ordered(step):
@@ -171,14 +200,18 @@
 
 
 def all_forward(layers, *refs):
-    (flag, tokens, cotangent, small, vectors, wi_own, wo_own, we_own, ws_own), refs = refs[:9], refs[9:]
+    (flag, tokens, cotangent, query_bias, value_bias, expand_bias), refs = refs[:6], refs[6:]
+    gains, refs = refs[:6], refs[6:]
+    (wi_own, wo_own, we_own, ws_own), refs = refs[:4], refs[4:]
     (rows_ref, cotangent_in, flag_in), refs = refs[:3], refs[3:]
     kept = [refs[STATES * layer : STATES * (layer + 1)] for layer in range(layers)]
     refs = refs[STATES * layers :]
     states = [refs[STATES * layer : STATES * (layer + 1)] for layer in range(layers)]
     refs = refs[STATES * layers :]
     tokens_in = states[0][16]
-    (save_sem, small_in, acc, rows_low, rows_in, local_sem, send_sem, recv_sem, kv_send, kv_recv, misc_send, misc_recv) = refs
+    biases = (query_bias, value_bias, expand_bias)
+    biases_in, refs = refs[:3], refs[3:]
+    (save_sem, acc, rows_low, local_sem, send_sem, recv_sem, kv_send, kv_recv, misc_send, misc_recv) = refs
     links = Links()
     core = links.core
     sems = (send_sem, recv_sem)
@@ -188,29 +221,45 @@
     weights = []
     for layer in range(layers):
         buffers = states[layer][:4]
+
+        def lanes(part, count):
+            return pl.ds(pl.multiple_of(part * count, 128), count)
+
         owns = [
-            lambda part, rows, layer=layer: wi_own.at[layer, part, rows],
-            lambda part, rows, layer=layer: wo_own.at[layer, part, rows],
-            lambda part, rows, layer=layer: we_own.at[layer, rows, pl.ds(pl.multiple_of(part * units, 128), units)],
-            lambda part, rows, layer=layer: ws_own.at[layer, part, rows],
+            lambda part, rows, kind, layer=layer: wi_own.at[layer, kind, rows, lanes(part, width)],
+            lambda part, rows, kind, layer=layer: wo_own.at[layer, part, rows],
+            lambda part, rows, kind, layer=layer: we_own.at[layer, rows, lanes(part, units)],
+            lambda part, rows, kind, layer=layer: ws_own.at[layer, part, rows],
         ]
-        weights.append([Weight(links, 4 * layer + number, owns[number], buffers[number], local_sem, sems) for number in range(4)])
+        weights.append([
+            Weight(links, 4 * layer + number, owns[number], 3 if number == 0 else 1, buffers[number], local_sem, sems)
+            for number in range(4)
+        ])
     every = [weight for group in weights for weight in group]
     for weight in every[:4]:
         weight.start_local()
-    links.greet([links.across, links.along, links.beside, links.opposite])
+    links.greet([links.across, links.along, links.along_next, links.beside, links.opposite])
     misc = (misc_send, misc_recv)
     swap_tokens = remote(tokens, tokens_in, misc, 0, links.opposite)
     swap_flag = remote(flag, flag_in, misc, 1, links.opposite)
-    copy_small = remote(small, small_in, misc, 2, links.across)
-    swap_cotangent = remote(cotangent, cotangent_in, misc, 3, links.opposite)
-    swap_rows = remote(rows_low, rows_in, misc, 4, links.opposite)
-    copy_small.start()
+    swap_cotangent = remote(cotangent, cotangent_in, misc, 2, links.opposite)
+    swap_rows = remote(rows_low, rows_ref, misc, 3, links.opposite)
+    copy_biases = [remote(biases[number], biases_in[number], misc, 4 + number, links.across) for number in range(3)]
 
     @pl.when(links.moved)
     def _():
+        swap_flag.start()
         swap_tokens.start()
-        swap_flag.start()
+
+    for copy in copy_biases:
+        copy.start()
+    every[0].start()
+
+    @pl.when(links.moved)
+    def _():
+        for weight in every[1:]:
+            weight.start()
+        swap_cotangent.start()
 
     @pl.when(jnp.logical_not(links.moved))
     def _():
@@ -218,28 +267,30 @@
         cotangent_in[...] = cotangent[...]
         flag_in[...] = flag[...]
 
-    for weight in every[:4]:
-        weight.start()
+    def start_rest():
+        @pl.when(jnp.logical_not(links.moved))
+        def _():
+            for weight in every[1:]:
+                weight.start()
+
+        for weight in every[4:]:
+            weight.start_local()
+
+    def bias(number, layer, index):
+        size = biases[number].shape[1] // 2
+        part = core + (index // 2) * (1 - 2 * core)
+        place = pl.ds(pl.multiple_of(part * size, 128), size)
+        return jnp.where(
+            lax.rem(index, 2) == 0, biases[number][layer : layer + 1, place], biases_in[number][layer : layer + 1, place]
+        )
 
     @pl.when(links.moved)
     def _():
-        swap_cotangent.start()
-
-    for weight in every[4:]:
-        weight.start()
-        weight.start_local()
-
-    def bias(layer, at, size, index):
-        part = core + (index // 2) * (1 - 2 * core)
-        place = pl.ds(pl.multiple_of(at + part * size, 128), size)
-        return jnp.where(lax.rem(index, 2) == 0, small[layer : layer + 1, place], small_in[layer : layer + 1, place])
-
-    @pl.when(links.moved)
-    def _():
+        swap_flag.wait_recv()
         swap_tokens.wait_recv()
-        swap_flag.wait_recv()
-
-    copy_small.wait_recv()
+
+    for copy in copy_biases:
+        copy.wait_recv()
     shift = jnp.where(flag_in[0:1, 0:1] < 0.5, 0.0, MASKED)
     acc[...] = tokens_in[...].astype(F32)
     halves = lane_halves((rows, width))
@@ -253,7 +304,7 @@
 
     for layer in range(layers):
         (wi, wo, we, ws, query_ref, pair_ref, remote_ref, mixed_ref, total_ref, normed_ref, first_ref, first_scale, active_ref, slope_ref, second_ref, second_scale, low_ref) = states[layer]
-        vector = lambda at: vectors[layer, at : at + 1]
+        vector = lambda at: gains[at][layer : layer + 1]
         wi_go, wo_go, we_go, ws_go = weights[layer]
         later = weights[layer + 1] if layer + 1 < layers else None
         if layer > 0:
@@ -265,38 +316,55 @@
         def project(step, carry):
             index = ordered(step)
             triple = dot(low_ref[...], wi[index])
-            query = (triple[:, :width] + bias(layer, 0, width, index)).astype(BF16)
+            query = (triple[:, :width] + bias(0, layer, index)).astype(BF16)
             query_ref[index] = query * BF16(DH ** (-0.5))
             pair_ref[index, :, :width] = triple[:, width : 2 * width].astype(BF16)
-            pair_ref[index, :, width:] = (triple[:, 2 * width :] + bias(layer, 2 * width, width, index)).astype(BF16)
+            pair_ref[index, :, width:] = (triple[:, 2 * width :] + bias(1, layer, index)).astype(BF16)
             exchange(index).start()
             return carry
 
+        def project_rest():
+            lax.fori_loop(2, 4, project, 0)
+
+        wi_go.wait_own()
+        lax.fori_loop(0, 2, project, 0)
+        after_pair = [[], [], [], []]
         if layer == 0:
             before_pair = [
-                [wi_go.relay],
-                [wo_go.relay, wi_go.relay_again],
-                [we_go.relay, wo_go.relay_again, wi_go.wait_fetched, lambda: lax.fori_loop(2, 4, project, 0)],
-                [ws_go.relay, we_go.relay_again],
+                [],
+                [wi_go.relay_again, wo_go.relay],
+                [wi_go.relay_last, wo_go.relay_again, we_go.relay, wi_go.wait_fetched, project_rest],
+                [wo_go.relay_last, we_go.relay_again, ws_go.relay],
             ]
-            before_quarter = [[later[0].relay, ws_go.relay_again], [later[1].relay, later[0].relay_again], [we_go.wait_fetched, ws_go.wait_fetched, later[1].relay_again], [later[2].relay]] if later else [[ws_go.relay_again], [], [we_go.wait_fetched, ws_go.wait_fetched], []]
-            wi_go.wait_own()
-            lax.fori_loop(0, 2, project, 0)
+            after_pair[0] = [start_rest, wi_go.relay]
+            before_feed = [we_go.relay_last, ws_go.relay_again, wo_go.wait_fetched]
+            before_quarter = [[], [ws_go.relay_last], [we_go.wait_fetched, ws_go.wait_fetched], []]
+            if later:
+                before_feed += [later[0].relay]
+                before_quarter[1] += [later[0].relay_again, later[1].relay]
+                before_quarter[2] += [later[2].relay]
+                before_quarter[3] += [later[0].relay_last, later[1].relay_again]
         else:
-            before_pair = [[ws_go.relay, we_go.relay_again], [], [ws_go.relay_again], []]
+            before_pair = [
+                [ws_go.relay, we_go.relay_again, wo_go.relay_last],
+                [ws_go.relay_again, we_go.relay_last],
+                [ws_go.relay_last, wi_go.wait_fetched, project_rest],
+                [],
+            ]
+            before_feed = [wo_go.wait_fetched]
             before_quarter = [[], [], [we_go.wait_fetched, ws_go.wait_fetched], []]
-            wi_go.wait_own()
-            wi_go.wait_fetched()
-            lax.fori_loop(0, 4, project, 0)
+            if later:
+                before_feed += [later[0].relay, later[1].relay]
+                before_quarter[2] += [later[0].relay_again, later[1].relay_again, later[2].relay]
+                before_quarter[3] += [later[0].relay_last]
         acc[...] += vector(0)
-        wo_go.wait_own()
-        before_pair[2].append(wo_go.wait_fetched)
 
         def one_pair(step, carry):
             at_step(step, before_pair)
             index = ordered(step)
             there = lax.rem(index + 2, 4)
             exchange(there).wait_recv()
+            at_step(step, after_pair)
             queries = query_ref[index]
             key_here, value_here = pair_ref[index, :, :width], pair_ref[index, :, width:]
             key_there, value_there = remote_ref[there, :, :width], remote_ref[there, :, width:]
@@ -317,10 +385,16 @@
             mixed_ref[index] = mixed_low
             totals = jnp.where(halves, total[0], total[1]).T
             total_ref[index] = jnp.concatenate([totals[0:8], totals[DH : DH + 8]], 0)
-            acc[...] += dot(mixed_low, wo[index])
             return carry
 
         lax.fori_loop(0, 4, one_pair, 0)
+        for action in before_feed:
+            action()
+        wo_go.wait_own()
+        total = acc[...]
+        for index in range(4):
+            total = total + dot(mixed_ref[index], wo[index])
+        acc[...] = total
         save(layer, 16, 0, 4, 5, 6, 1, 7, 8)
         first, scale = normalise(acc[...])
         first_ref[...] = first
@@ -335,7 +409,7 @@
         def one_quarter(step, carry):
             at_step(step, before_quarter)
             index = ordered(step)
-            active, slope = gelu_parts(dot(normed_ref[...], we[index]) + bias(layer, 4 * width, units, index))
+            active, slope = gelu_parts(dot(normed_ref[...], we[index]) + bias(2, layer, index))
             active_low = active.astype(BF16)
             active_ref[index] = active_low
             slope_ref[index] = slope.astype(BF16)
@@ -355,20 +429,20 @@
     @pl.when(links.moved)
     def _():
         swap_rows.start()
-        swap_rows.wait_recv()
-        rows_ref[...] = rows_in[...].astype(F32)
 
     @pl.when(jnp.logical_not(links.moved))
     def _():
-        rows_ref[...] = acc[...]
+        rows_ref[...] = rows_low[...]
 
     @pl.when(links.moved)
     def _():
-        swap_cotangent.wait_recv()
+        for copy in (swap_cotangent, swap_rows):
+            copy.wait_recv()
         for copy in (swap_tokens, swap_flag, swap_cotangent, swap_rows):
             copy.wait_send()
 
-    copy_small.wait_send()
+    for copy in copy_biases:
+        copy.wait_send()
     for weight in every:
         weight.wait_sent()
     for layer in range(layers):
@@ -395,10 +469,21 @@
     return 3 - ordered(step)
 
 
+GRADIENT_LANES = (
+    ((1, 0, 4), (-1, 1, 4), (1, 2, 4), (-1, 3, 4)),
+    ((-1, 0, 1),),
+    ((1, 0, 3), (-1, 1, 3), (1, 2, 3)),
+)
+
+
+def lanes_of(kind, columns):
+    return [(way, at * columns // parts, columns // parts) for way, at, parts in GRADIENT_LANES[kind]]
+
+
 class Gradient:
-    def __init__(self, links, number, mine, theirs, core_in, narrow_in, slots, further_in, out, columns, sems):
+    def __init__(self, links, number, mine, theirs, core_in, narrow_in, slots, further_in, out, lanes, sems):
         self.links, self.number, self.mine, self.theirs, self.core_in = links, number, mine, theirs, core_in
-        self.narrow_in, self.slots, self.further_in, self.out, self.columns, self.sems = narrow_in, slots, further_in, out, columns, sems
+        self.narrow_in, self.slots, self.further_in, self.out, self.lanes, self.sems = narrow_in, slots, further_in, out, lanes, sems
         self.size = core_in.shape[1]
         self.piece = mine.shape[1] // links.chips
 
@@ -412,23 +497,23 @@
         place = self.out.at[self.links.core]
         return remote(place, place, self.sems[0], (self.number, 3), self.links.beside)
 
-    def ring_copy(self, side, step):
-        links, way = self.links, 1 - 2 * side
-        at, count = self.columns[side]
-        device = links.right if side == 0 else links.left
-        where = (self.number, side, step)
+    def ring_copy(self, lane, step):
+        links = self.links
+        way, at, count = self.lanes[lane]
+        device = links.right if way > 0 else links.left
+        where = (self.number, lane, step)
         if step < links.chips - 1:
             source = self.mine.at[0, self.rows(-way * step), pl.ds(at, count)]
-            return remote(source, self.slots[side].at[step], self.sems[1], where, device)
+            return remote(source, self.slots[lane].at[step], self.sems[1], where, device)
         rows = self.rows(-way * (step - links.chips))
         target = self.out.at[links.core, rows, pl.ds(at, count)]
         source = self.mine.at[0, rows, pl.ds(at, count)] if step == links.chips - 1 else target
         return remote(source, target, self.sems[1], where, device)
 
-    def further_copy(self, side, number):
-        at, count = self.columns[side]
-        source = self.mine.at[0, self.rows(1 - 2 * side), pl.ds(at, count)]
-        return remote(source, self.further_in[side].at[number], self.sems[2], (self.number, side, number), self.links.further[number])
+    def further_copy(self, lane, number):
+        way, at, count = self.lanes[lane]
+        source = self.mine.at[0, self.rows(way), pl.ds(at, count)]
+        return remote(source, self.further_in[lane].at[number], self.sems[2], (self.number, lane, number), self.links.further[number])
 
     def rows(self, offset):
         index = lax.rem(self.links.place + offset + 2 * self.links.chips, self.links.chips)
@@ -448,30 +533,28 @@
         self.narrow_copy().wait_recv()
         total = self.mine[0, 0 : self.size].astype(F32) + self.core_in[0].astype(F32) + self.narrow_in[...].astype(F32)
         self.mine[0, 0 : self.size] = total.astype(BF16)
-        for side in range(2):
-            self.ring_copy(side, 0).start()
+        for lane in range(len(self.lanes)):
+            self.ring_copy(lane, 0).start()
 
     def tick(self, step):
         chips = self.links.chips
-        for side in range(2):
-            way = 1 - 2 * side
-            at, count = self.columns[side]
-            self.ring_copy(side, step).wait_recv()
+        for lane, (way, at, count) in enumerate(self.lanes):
+            self.ring_copy(lane, step).wait_recv()
             if step < chips - 1:
                 rows = self.rows(-way * (step + 1))
-                total = self.mine[0, rows, at : at + count].astype(F32) + self.slots[side][step].astype(F32)
+                total = self.mine[0, rows, at : at + count].astype(F32) + self.slots[lane][step].astype(F32)
                 total = total.astype(BF16)
                 self.mine[0, rows, at : at + count] = total
                 for number in range(len(self.links.further) if step == chips - 2 else 0):
-                    copy = self.further_copy(side, number)
+                    copy = self.further_copy(lane, number)
                     copy.start()
                     copy.wait()
-                    total = (total.astype(F32) + self.further_in[side][number].astype(F32)).astype(BF16)
+                    total = (total.astype(F32) + self.further_in[lane][number].astype(F32)).astype(BF16)
                     self.mine[0, rows, at : at + count] = total
                 if step == chips - 2:
                     self.out[self.links.core, rows, at : at + count] = total
             if step < 2 * chips - 3:
-                self.ring_copy(side, step + 1).start()
+                self.ring_copy(lane, step + 1).start()
 
     def share(self):
         self.share_copy().start()
@@ -486,24 +569,31 @@
         if not theirs_waited:
             self.free_theirs()
         self.narrow_copy().wait_send()
-        for side in range(2):
+        for lane in range(len(self.lanes)):
             for step in range(2 * self.links.chips - 2):
-                self.ring_copy(side, step).wait_send()
+                self.ring_copy(lane, step).wait_send()
 
 
 def all_backward(layers, chips, *refs):
-    (flag, vectors, cotangent), refs = refs[:3], refs[3:]
+    (flag, cotangent), refs = refs[:2], refs[2:]
+    gains, refs = refs[:6], refs[6:]
     kept = [refs[STATES * layer : STATES * (layer + 1)] for layer in range(layers)]
     refs = refs[STATES * layers :]
     (rows_ref, small_out), refs = refs[:2], refs[2:]
-    outs = [refs[3 * layer : 3 * layer + 3] for layer in range(layers)]
-    refs = refs[3 * layers :]
+    outs = [[ref.at[layer] for ref in refs[:3]] for layer in range(layers)]
+    refs = refs[3:]
     state, refs = refs[:STATES], refs[STATES:]
-    (acc, turned, summed_ref, mixed_grad_ref, inner_ref, query_grad_ref, here_ref, away_ref, rows_low, rows_in), refs = refs[:10], refs[10:]
+    (acc, turned, summed_ref, mixed_grad_ref, inner_ref, query_grad_ref, here_ref, away_ref, rows_low), refs = refs[:9], refs[9:]
     away_in, refs = refs[:layers], refs[layers:]
     theirs, refs = refs[:3], refs[3:]
-    buffers = [refs[21 * layer : 21 * layer + 21] for layer in range(layers)]
-    refs = refs[21 * layers :]
+    buffers = []
+    for layer in range(layers):
+        group = []
+        for lanes in GRADIENT_LANES:
+            count = len(lanes)
+            group.append((refs[0], refs[1], refs[2], refs[3 : 3 + count], refs[3 + count : 3 + 2 * count]))
+            refs = refs[3 + 2 * count :]
+        buffers.append(group)
     (small, core_small, mid_small, row_small, sum_small, step_small), refs = refs[:6], refs[6:]
     (load_sem, away_send, away_recv, grad_send, grad_recv, ring_send, ring_recv, misc_send, misc_recv, step_send, step_recv, further_send, further_recv) = refs
     (wi, wo, we, ws, query, pair, remote_pair, mixed, total_ref, normed, first, first_scale, active, slope, second, second_scale, hidden_low) = state
@@ -534,16 +624,10 @@
     for layer in range(layers):
         group = []
         for kind in range(3):
-            mine, core_in, narrow_in, slot_one, slot_two, further_one, further_two = buffers[layer][7 * kind : 7 * kind + 7]
-            if kind < 2:
-                half = mine.shape[2] // 2
-                columns = ((0, half), (half, half))
-            else:
-                third = mine.shape[2] // 3
-                columns = ((0, 2 * third), (2 * third, third))
+            mine, core_in, narrow_in, slots, further_in = buffers[layer][kind]
             group.append(Gradient(
-                links, 3 * layer + kind, mine, theirs[kind], core_in, narrow_in, (slot_one, slot_two), (further_one, further_two), outs[layer][kind], columns,
-                ((grad_send, grad_recv), (ring_send, ring_recv), (further_send, further_recv)),
+                links, 3 * layer + kind, mine, theirs[kind], core_in, narrow_in, slots, further_in, outs[layer][kind],
+                lanes_of(kind, mine.shape[2]), ((grad_send, grad_recv), (ring_send, ring_recv), (further_send, further_recv)),
             ))
         gradients.append(group)
     rows, width = mixed.shape[1], mixed.shape[2]
@@ -558,7 +642,7 @@
     for layer in reversed(range(layers)):
         feed, output, inputs = gradients[layer]
         before = gradients[layer + 1] if layer + 1 < layers else None
-        vector = lambda at: vectors[layer, at : at + 1]
+        vector = lambda at: gains[at][layer : layer + 1]
 
         def put(gradient, index, at, value):
             @pl.when(index < 2)
@@ -584,11 +668,11 @@
         if before:
             for gradient in before:
                 gradient.free_theirs()
-        block_hooks = [[], [functools.partial(feed.send, 1)], [feed.middle], [functools.partial(feed.send, 0)]]
+        block_hooks = [[], [functools.partial(feed.send, 1)], [], [functools.partial(feed.send, 0), feed.middle]]
         if before:
             block_hooks[0].append(before[0].settle)
-            for number in range(3):
-                block_hooks[number + 1].append(tick(0, number))
+            block_hooks[1].append(tick(0, 0))
+            block_hooks[3].append(tick(0, 1))
 
         def one_quarter(step, carry):
             at_step(step, block_hooks)
@@ -612,8 +696,9 @@
         summed_ref[...] = summed
         rows_low[...] = summed.astype(BF16)
         if before:
-            before[0].tick(3)
+            before[0].tick(2)
             before[1].settle()
+            before[2].settle()
 
         def one_output(step, carry):
             index = backwards(step)
@@ -633,11 +718,16 @@
             load(layer - 1, block_group)
         loaded(layer, *pair_group)
         pair_hooks = [[], [output.middle], [], []]
+        middle_hooks = [[], [], [], []]
         if before:
-            pair_hooks[0] += [tick(0, 4), before[2].settle]
-            pair_hooks[1] += [tick(0, 5), tick(1, 0), tick(2, 0)]
-            pair_hooks[2] += [tick(0, 6), tick(1, 1), tick(2, 1)]
-            pair_hooks[3] += [tick(0, 7), tick(1, 2), tick(2, 2)]
+            both = lambda step: [tick(1, step), tick(2, step)]
+            pair_hooks[0] += [tick(0, 3)] + both(0)
+            pair_hooks[1] += [tick(0, 4)] + both(1)
+            middle_hooks[1] += [tick(0, 5)] + both(2)
+            pair_hooks[2] += [tick(0, 6)] + both(3)
+            middle_hooks[2] += [tick(0, 7)] + both(4)
+            pair_hooks[3] += [tick(0, 8)] + both(5)
+            middle_hooks[3] += [tick(0, 9)] + both(6)
 
         def away_copy(there):
             return remote(away_ref.at[there], away_in[layer].at[there], (away_send, away_recv), (layer, there), links.beside)
@@ -653,6 +743,8 @@
             queries, grads = query[index], mixed_grad_ref[index]
             query_turned = None
             for side in range(2):
+                if side == 1:
+                    at_step(step, middle_hooks)
                 source, place = (pair, index) if side == 0 else (remote_pair, there)
                 keys, values = source[place, :, :width], source[place, :, width:]
                 key_grad = value_grad = None
@@ -691,10 +783,10 @@
         acc[...] = summed_ref[...]
         input_hooks = [[], [functools.partial(inputs.send, 1)], [inputs.middle], [functools.partial(inputs.send, 0)]]
         if before:
-            input_hooks[0] += [tick(0, 8)]
-            input_hooks[1] += [tick(1, 3), tick(2, 3)]
-            input_hooks[2] += [tick(0, 9)]
-            input_hooks[3] += [tick(1, 4), tick(2, 4)]
+            feed.settle()
+            input_hooks[0] += [tick(0, 10)] + both(7)
+            input_hooks[2] += [tick(0, 11)] + both(8)
+            input_hooks[3] += [functools.partial(feed.tick, 0)]
 
         def one_input(step, carry):
             at_step(step, input_hooks)
@@ -713,7 +805,7 @@
 
     feed, output, inputs = gradients[0]
     rows_low[...] = acc[...].astype(BF16)
-    swap_rows = remote(rows_low, rows_in, misc, 0, links.opposite)
+    swap_rows = remote(rows_low, rows_ref, misc, 0, links.opposite)
     copy_core = remote(small.at[pl.ds(2, 2)], core_small, misc, 1, links.beside)
     copy_row = remote(mid_small, row_small, misc, 2, links.across)
     share_small = remote(small_out.at[core], small_out.at[core], misc, 3, links.beside)
@@ -722,28 +814,29 @@
         return remote(sum_small.at[step], step_small.at[step], (step_send, step_recv), step, bits[step])
 
     copy_core.start()
+    copy_core.wait_recv()
+    mid_small[...] = small[1] + core_small[1]
+    copy_row.start()
 
     @pl.when(links.moved)
     def _():
         swap_rows.start()
 
-    copy_core.wait_recv()
-    mid_small[...] = small[1] + core_small[1]
-    copy_row.start()
     ticks = 2 * links.chips - 2
     queues = []
     if layers > 1:
-        queues += [(0, gradients[1][0], 10), (0, gradients[1][1], 5), (0, gradients[1][2], 5)]
-    feed_at, late_at = 0, 3
-    queues += [(feed_at + 1, feed, 0), (late_at + 1, output, 0), (late_at + 1, inputs, 0)]
-    for gradient in gradients[2:]:
-        pass
+        queues += [(0, gradients[1][0], 12), (0, gradients[1][1], 9), (0, gradients[1][2], 9)]
+    late_at, small_at = 3, 4
+    started = 1
+    if layers == 1:
+        feed.settle()
+        started = 0
+    queues += [(0, feed, started), (1, output, 0), (late_at + 1, inputs, 0)]
     value = None
     for step in range(late_at + 1 + ticks):
-        if step == feed_at:
-            feed.settle()
+        if step == 0:
+            output.settle()
         if step == late_at:
-            output.settle()
             inputs.settle()
         for start, gradient, done in queues:
             at = step - start + done
@@ -751,16 +844,16 @@
                 gradient.tick(at)
                 if at == ticks - 1:
                     gradient.share()
-        if step == 1:
+        if step == small_at:
             copy_row.wait_recv()
             value = small[0] + core_small[0] + row_small[...]
-        if 1 < step <= steps + 1:
-            step_copy(step - 2).wait_recv()
-            value = value + step_small[step - 2]
-        if 1 <= step <= steps:
-            sum_small[step - 1] = value
-            step_copy(step - 1).start()
-        if step == steps + 1:
+        if small_at < step <= small_at + steps:
+            step_copy(step - small_at - 1).wait_recv()
+            value = value + step_small[step - small_at - 1]
+        if small_at <= step < small_at + steps:
+            sum_small[step - small_at] = value
+            step_copy(step - small_at).start()
+        if step == small_at + steps:
             small_out[core] = value
             share_small.start()
 
@@ -768,11 +861,10 @@
     def _():
         swap_rows.wait_recv()
         swap_rows.wait_send()
-        rows_ref[...] = rows_in[...].astype(F32)
 
     @pl.when(jnp.logical_not(links.moved))
     def _():
-        rows_ref[...] = acc[...]
+        rows_ref[...] = rows_low[...]
 
     share_small.wait_recv()
     share_small.wait_send()
@@ -788,18 +880,29 @@
 
 
 def assemble_kernel(layers, *refs):
-    ins, refs = refs[: 3 * layers], refs[3 * layers :]
-    (shrink_ref, expand_ref, output_ref, input_ref) = refs
-    for layer in range(layers):
-        feed, output, inputs = ins[3 * layer : 3 * layer + 3]
-        units, depth = expand_ref.shape[2] // 2, expand_ref.shape[1]
-        width = output_ref.shape[1] // 2
-        for part in range(2):
-            shrink_ref[layer, part * units : (part + 1) * units] = feed[part, 0:units].astype(F32)
-            expand_ref[layer, :, part * units : (part + 1) * units] = feed[part, units : units + depth].astype(F32)
-            output_ref[layer, part * width : (part + 1) * width] = output[part, 0:width].astype(F32)
-            for kind in range(3):
-                input_ref[kind, layer, :, part * width : (part + 1) * width] = inputs[part, 0:depth, kind * width : (kind + 1) * width].astype(F32)
+    (feed, output, inputs, small, out_rows, in_rows), refs = refs[:6], refs[6:]
+    (shrink_ref, expand_ref, output_ref, input_ref, out_rows_ref, in_rows_ref), refs = refs[:6], refs[6:]
+    vector_refs, (expand_bias_ref, query_bias_ref, value_bias_ref) = refs[:6], refs[6:]
+    units, depth, width = shrink_ref.shape[1], shrink_ref.shape[2], output_ref.shape[1]
+    shrink_ref[0] = feed[0, 0, 0:units].astype(F32)
+    expand_ref[0] = feed[0, 0, units : units + depth].astype(F32)
+    output_ref[0] = output[0, 0, 0:width].astype(F32)
+    for kind in range(3):
+        input_ref[0, kind] = inputs[0, 0, 0:depth, kind * width : (kind + 1) * width].astype(F32)
+    out_rows_ref[...] = out_rows[...].astype(F32)
+    in_rows_ref[...] = in_rows[...].astype(F32)
+
+    @pl.when(pl.program_id(0) + pl.program_id(1) == 0)
+    def _():
+        for layer in range(layers):
+            for number in range(6):
+                vector_refs[number][layer : layer + 1] = small[0, 8 * layer + number : 8 * layer + number + 1]
+            for part in range(2):
+                row = slice(8 * layer + 6, 8 * layer + 7)
+                expand_bias_ref[layer : layer + 1, part * units : (part + 1) * units] = small[part, row, 0:units]
+                row = slice(8 * layer + 7, 8 * layer + 8)
+                query_bias_ref[layer : layer + 1, part * width : (part + 1) * width] = small[part, row, 0:width]
+                value_bias_ref[layer : layer + 1, part * width : (part + 1) * width] = small[part, row, 2 * width : 3 * width]
 
 
 VM = pl.BlockSpec(memory_space=pltpu.VMEM)
@@ -826,15 +929,11 @@
     units = expand_weight.shape[2] // 2
 
     flag = jnp.broadcast_to(bucket, (8, 128)).astype(F32)
-    input_own = (
-        input_weight.reshape(layers, depth, 3, 2, width).transpose(0, 3, 1, 2, 4).reshape(layers, 2, depth, 3 * width)
-    )
+    input_own = input_weight.transpose(0, 2, 1, 3)
     output_own = output_weight.reshape(layers, 2, width, depth)
     shrink_own = shrink_weight.reshape(layers, 2, units, depth)
-    small = jnp.concatenate([query_bias, value_bias, expand_bias], 1)
-    vectors = jnp.stack(
-        [output_bias, first_gain, first_shift, shrink_bias, second_gain, second_shift, output_bias, output_bias], 1
-    )
+    gains = (output_bias, first_gain, first_shift, shrink_bias, second_gain, second_shift)
+    biases = (query_bias, value_bias, expand_bias)
     query_shape = shaped(BF16, 4, rows, width)
     pair_shape = shaped(BF16, 4, rows, 2 * width)
     row_shape = shaped(F32, rows, depth)
@@ -850,50 +949,51 @@
     kept_shapes = state_shapes * layers
     results = pl.pallas_call(
         functools.partial(all_forward, layers),
-        out_shape=[row_shape, low_shape, shaped(F32, 8, 128)] + kept_shapes,
-        in_specs=[VM] * 5 + [AN] * 4,
+        out_shape=[low_shape, low_shape, shaped(F32, 8, 128)] + kept_shapes,
+        in_specs=[VM] * 12 + [AN] * 4,
         out_specs=[VM] * 3 + [AN] * len(kept_shapes),
-        scratch_shapes=state_scratch * layers + [
+        scratch_shapes=state_scratch * layers + [pltpu.VMEM(bias.shape, F32) for bias in biases] + [
             pltpu.SemaphoreType.DMA((layers, STATES)),
-            pltpu.VMEM(small.shape, F32), pltpu.VMEM((rows, depth), F32), pltpu.VMEM((rows, depth), BF16), pltpu.VMEM((rows, depth), BF16),
-            pltpu.SemaphoreType.DMA((8 * layers,)),
-            pltpu.SemaphoreType.DMA((16 * layers,)), pltpu.SemaphoreType.DMA((16 * layers,)),
+            pltpu.VMEM((rows, depth), F32), pltpu.VMEM((rows, depth), BF16),
+            pltpu.SemaphoreType.DMA((4 * layers, 6)),
+            pltpu.SemaphoreType.DMA((4 * layers, 10)), pltpu.SemaphoreType.DMA((4 * layers, 10)),
             pltpu.SemaphoreType.DMA((layers, 4)), pltpu.SemaphoreType.DMA((layers, 4)),
-            pltpu.SemaphoreType.DMA((5,)), pltpu.SemaphoreType.DMA((5,)),
+            pltpu.SemaphoreType.DMA((7,)), pltpu.SemaphoreType.DMA((7,)),
         ],
         compiler_params=pltpu.CompilerParams(collective_id=1, has_side_effects=True, vmem_limit_bytes=62 * 2**20),
         cost_estimate=cost(10**10, 10**8),
         name="forward",
-    )(flag, tokens, cotangent, small, vectors, input_own, output_own, expand_weight, shrink_own)
-    layer_output, cotangent, flag = results[:3]
+    )(flag, tokens, cotangent, *biases, *gains, input_own, output_own, expand_weight, shrink_own)
+    out_rows, cotangent, flag = results[:3]
     chips = wide // 2
     ring = ring_size(chips)
     further = (chips // ring).bit_length() - 1
     tall = lambda size: -(-size // (16 * ring)) * 16 * ring
     out_shapes, buffer_scratch, theirs_scratch = [], [], []
-    for size, columns, first_columns in ((units + depth, depth, depth // 2), (width, depth, depth // 2), (depth, 3 * width, 2 * width)):
-        out_shapes.append(shaped(BF16, 2, tall(size), columns))
+    for kind, (size, columns) in enumerate(((units + depth, depth), (width, depth), (depth, 3 * width))):
+        out_shapes.append(shaped(BF16, layers, 2, tall(size), columns))
         theirs_scratch.append(pltpu.VMEM((2, size, columns), BF16))
         slot = lambda count: pltpu.VMEM((ring - 1, tall(size) // ring, count), BF16)
         more = lambda count: pltpu.VMEM((further, tall(size) // ring, count) if further else (1, 16, 128), BF16)
         buffer_scratch += [
             pltpu.VMEM((2, tall(size), columns), BF16), pltpu.VMEM((2, size, columns), BF16), pltpu.VMEM((size, columns), BF16),
-            slot(first_columns), slot(columns - first_columns), more(first_columns), more(columns - first_columns),
         ]
+        lanes = lanes_of(kind, columns)
+        buffer_scratch += [slot(count) for way, at, count in lanes] + [more(count) for way, at, count in lanes]
     small_rows = 8 * layers
     steps = chips.bit_length() - 1
     small_scratch = pltpu.VMEM((small_rows, depth), F32)
-    ring_sem = pltpu.SemaphoreType.DMA((3 * layers, 2, 2 * ring - 2))
-    further_sem = pltpu.SemaphoreType.DMA((3 * layers, 2, max(further, 1)))
+    ring_sem = pltpu.SemaphoreType.DMA((3 * layers, 4, 2 * ring - 2))
+    further_sem = pltpu.SemaphoreType.DMA((3 * layers, 4, max(further, 1)))
     results = pl.pallas_call(
         functools.partial(all_backward, layers, chips),
-        out_shape=[row_shape, shaped(F32, 2, small_rows, depth)] + out_shapes * layers,
-        in_specs=[VM] * 3 + [AN] * len(kept_shapes),
-        out_specs=[VM] * (2 + 3 * layers),
+        out_shape=[low_shape, shaped(F32, 2, small_rows, depth)] + out_shapes,
+        in_specs=[VM] * 8 + [AN] * len(kept_shapes),
+        out_specs=[VM] * 5,
         scratch_shapes=state_scratch + [
             pltpu.VMEM((rows, depth), F32), pltpu.VMEM((depth, rows), BF16), pltpu.VMEM((rows, depth), F32),
             pltpu.VMEM(query_shape.shape, BF16), pltpu.VMEM(stat_shape.shape, F32), pltpu.VMEM(query_shape.shape, BF16),
-            pltpu.VMEM(pair_shape.shape, F32), pltpu.VMEM(pair_shape.shape, BF16), pltpu.VMEM((rows, depth), BF16), pltpu.VMEM((rows, depth), BF16),
+            pltpu.VMEM(pair_shape.shape, F32), pltpu.VMEM(pair_shape.shape, BF16), pltpu.VMEM((rows, depth), BF16),
         ] + [pltpu.VMEM(pair_shape.shape, BF16)] * layers + theirs_scratch + buffer_scratch * layers + [
             pltpu.VMEM((4, small_rows, depth), F32), pltpu.VMEM((2, small_rows, depth), F32), small_scratch, small_scratch,
             pltpu.VMEM((steps, small_rows, depth), F32), pltpu.VMEM((steps, small_rows, depth), F32),
@@ -907,39 +1007,48 @@
         compiler_params=pltpu.CompilerParams(collective_id=0, has_side_effects=True, vmem_limit_bytes=67043328),
         cost_estimate=cost(10**10, 10**8),
         name="backward",
-    )(flag, vectors, cotangent, *results[3:])
-    input_rows, small = results[:2]
-    shrink_grad, expand_grad, output_grad, input_grad = pl.pallas_call(
+    )(flag, cotangent, *gains, *results[3:])
+    in_rows, small = results[:2]
+    whole = lambda *dims: pl.BlockSpec(dims, lambda layer, part: (0,) * len(dims))
+    piece = lambda shape: pl.BlockSpec((1, 1) + shape.shape[2:], lambda layer, part: (layer, part, 0, 0))
+    strip = pl.BlockSpec((rows // (2 * layers), depth), lambda layer, part: (2 * layer + part, 0))
+    upright = lambda size: pl.BlockSpec((1, size, depth), lambda layer, part: (layer, part, 0))
+    vector_shape = shaped(F32, layers, depth)
+    outs = pl.pallas_call(
         functools.partial(assemble_kernel, layers),
+        grid=(layers, 2),
         out_shape=[
             shaped(F32, layers, 2 * units, depth), shaped(F32, layers, depth, 2 * units), shaped(F32, layers, 2 * width, depth),
-            shaped(F32, 3, layers, depth, 2 * width),
-        ],
-        in_specs=[VM] * (3 * layers),
-        out_specs=[VM] * 4,
+            shaped(F32, layers, 3, depth, 2 * width), row_shape, row_shape,
+        ] + [vector_shape] * 6 + [shaped(F32, layers, 2 * units), shaped(F32, layers, 2 * width), shaped(F32, layers, 2 * width)],
+        in_specs=[piece(shape) for shape in out_shapes] + [whole(2, small_rows, depth), strip, strip],
+        out_specs=[
+            upright(units), pl.BlockSpec((1, depth, units), lambda layer, part: (layer, 0, part)), upright(width),
+            pl.BlockSpec((1, 3, depth, width), lambda layer, part: (layer, 0, 0, part)), strip, strip,
+        ] + [whole(layers, depth)] * 6 + [whole(layers, 2 * units), whole(layers, 2 * width), whole(layers, 2 * width)],
         compiler_params=pltpu.CompilerParams(vmem_limit_bytes=40 * 2**20),
         cost_estimate=cost(10**6, 2 * 10**7),
         name="assemble",
-    )(*results[2:])
-    small = small.reshape(2, layers, 8, depth)
-    both = lambda at, a, b: small[:, :, at, a:b].transpose(1, 0, 2).reshape(layers, 2 * (b - a))
-    vector = lambda at: small[0, :, at]
+    )(*results[2:], small, out_rows, in_rows)
+    shrink_grad, expand_grad, output_grad, input_grad, layer_output, input_rows = outs[:6]
+    second_shift_grad, second_gain_grad, shrink_bias_grad, first_shift_grad, first_gain_grad, output_bias_grad = outs[6:12]
+    expand_bias_grad, query_bias_grad, value_bias_grad = outs[12:]
     return (
         layer_output,
         input_rows,
-        input_grad.transpose(1, 2, 0, 3),
-        both(7, 0, width),
-        both(7, 2 * width, 3 * width),
+        input_grad.transpose(0, 2, 1, 3),
+        query_bias_grad,
+        value_bias_grad,
         output_grad,
-        vector(5),
-        vector(4),
-        vector(3),
+        output_bias_grad,
+        first_gain_grad,
+        first_shift_grad,
         expand_grad,
-        both(6, 0, units),
+        expand_bias_grad,
         shrink_grad,
-        vector(2),
-        vector(1),
-        vector(0),
+        shrink_bias_grad,
+        second_gain_grad,
+        second_shift_grad,
     )
 
 

time: 270 us -> 255 us (0.944)
  local copies, waits for them, and re-layouts: 26.3 us -> 8.15 us
  Pallas kernels: 240 us -> 245 us
    unnamed x21 -> x12, local copies, waits for them, and re-layouts: 14.3 us -> 7.55 us
    pallas_call x2, Pallas kernels: 85.4 us -> 90.9 us  [the longest x1 85.4 us: local(): pl.pallas_call(functools.partial(all_forward, layers), out_shape=[low_sha...]
    another operation x7 -> x0, local copies, waits for them, and re-layouts: 4.8 us -> none  [local(): jnp.stack([output_bias, first_gain, first_shift, shrink_bias, second_gain...]
    slice x3 -> x0, local copies, waits for them, and re-layouts: 3.17 us -> none  [the longest x2 2.17 us: local(): small[:, :, at, a:b].transpose(1, 0, 2).reshape(layers, 2 * (b - a))]
where the time goes in v1:
time: 255 us
  Pallas kernels  245 us (96%)
  local copies, waits for them, and re-layouts  8.15 us (3%)
    pallas_call x1, Pallas kernels, local(): pl.pallas_call(functools.partial(all_backward, layers, chips), out_shape=...  154 us
    pallas_call x1, Pallas kernels, local(): pl.pallas_call(functools.partial(all_forward, layers), out_shape=[low_sha...  85.4 us
    unnamed x12, local copies, waits for them, and re-layouts  7.55 us
    pallas_call x1, Pallas kernels, local(): pl.pallas_call(functools.partial(assemble_kernel, layers), grid=(layers,...  5.47 us

profile of v1, /device:TPU:0, one launch (start us, length us, event | category | flops | bytes accessed | tf_op | source)
XLA Modules:
  0.0 255.0 jit_solution(3622397158555797577)
XLA Ops:
  1.3 0.6 broadcast_in_dim.2.refs_0_
  1.9 85.4 %forward.1 = (bf16[512,512]{1,0:T(8,128)(2,1)}, bf16[512,512]{1,0:T(8,128)(2,1)}, f32[8,128]{1,0:T(8,128)}, bf16[4,512,384]{2,1,0:T(8,128)(2,1)}, bf16[4,128,512...) custom-call(f32[8,128]{1,0:T(8,128)} %broadcast_in_dim.2.refs_0_, ...), custom_call_target="tpu_custom_call" | custom-call | flops 10000000000 | bytes 100000000 | tf_op jit(solution)/shard_map/forward/pallas_call | solution.py:950
  87.3 154.5 %backward.1 = (bf16[512,512]{1,0:T(8,128)(2,1)}, f32[2,16,512]{2,1,0:T(8,128)}, bf16[2,2,1024,512]{3,2,1,0:T(8,128)(2,1)}, bf16[2,2,128,512]{3,2,1,0:T(8,128)(2,1)}, bf16[2,2,512,384]{3,2,1,0:T(8,128)(2,1)}) custom-call(f32[8,128]{1,0:T(8,128)} %get-tuple-element.72.refs_0_, bf16[512,512]{1,0:T(8,128)(2,1)} %get-tuple-element.73.refs_1_, f32[2,512]{1,0:T(2,128)} %refs_2_.3, ...), custom_call_target="tpu_custom_call" | custom-call | flops 10000000000 | bytes 100000000 | tf_op jit(solution)/shard_map/backward/pallas_call | solution.py:988
  241.8 0.0 copy-start
  241.8 2.2 copy-done
  244.0 0.0 copy-start.1
  244.0 1.4 copy-done.1
  245.4 0.0 copy-start.2
  245.4 1.0 copy-done.2
  246.5 0.0 copy-start.3
  246.5 1.0 copy-done.3
  247.5 0.0 copy-start.4
  247.5 1.0 copy-done.4
  248.6 0.0 copy-start.5
  248.6 0.8 copy-done.5
  249.4 5.5 %assemble.1 = (f32[2,1024,512]{2,1,0:T(8,128)}, f32[2,512,1024]{2,1,0:T(8,128)}, f32[2,256,512]{2,1,0:T(8,128)}, f32[2,3,512,256]{3,2,1,0:T(8,128)}, f32[512,512...) custom-call(bf16[2,2,1024,512]{3,2,1,0:T(8,128)(2,1)S(1)} %copy-done, ...), custom_call_target="tpu_custom_call" | custom-call | flops 1000000 | bytes 20000000 | tf_op jit(solution)/shard_map/assemble/pallas_call | solution.py:1017
Async XLA Ops:
  241.8 2.2 copy-start
  244.0 1.4 copy-start.1
  245.4 1.0 copy-start.2
  246.5 1.0 copy-start.3
  247.5 1.0 copy-start.4
  248.6 0.8 copy-start.5

commit v2 on v1

--- a/solution.py
+++ b/solution.py
@@ -14,6 +14,7 @@
 F32 = jnp.float32
 BF16 = jnp.bfloat16
 STATES = 17
+KINDS = 5
 
 
 def dot(a, b):
@@ -50,10 +51,6 @@
     tail = poly * square
     phi = jnp.where(a >= 0, 1.0 - tail, tail)
     return a * phi, phi + a * square * 0.3989422804014327
-
-
-def ring_size(chips):
-    return min(chips, 8)
 
 
 class Links:
@@ -71,24 +68,18 @@
         self.opposite = (other_core, other_narrow)
         self.moved = self.core + self.narrow == 1
 
-    def ring(self, chips):
-        self.chips = ring_size(chips)
-        self.group = self.chip // self.chips
-        at = lax.rem(self.chip, self.chips)
-        odd = lax.rem(at, 2)
-        self.place = odd * (self.chips - 1 - at // 2) + (1 - odd) * (at // 2)
-        self.right, self.left = self.ring_device(1), self.ring_device(-1)
+    def plane(self, chips):
+        assert chips % 8 == 0
+        self.line = lax.rem(self.chip // 2, 4)
+        self.line_peers = []
+        for offset in range(1, 4):
+            there = lax.rem(self.line + offset, 4)
+            self.line_peers.append((self.wide + 4 * (there - self.line), self.narrow))
         self.bits = []
         for bit in range(chips.bit_length() - 1):
             side = lax.rem(self.chip // 2**bit, 2)
             self.bits.append((self.wide + 2 ** (bit + 1) * (1 - 2 * side), self.narrow))
-        self.further = self.bits[self.chips.bit_length() - 1 :]
-
-    def ring_device(self, offset):
-        place = lax.rem(self.place + offset + self.chips, self.chips)
-        late = place // (self.chips // 2)
-        chip = late * (2 * (self.chips - 1 - place) + 1) + (1 - late) * (2 * place)
-        return (2 * (self.group * self.chips + chip) + self.core, self.narrow)
+        self.further = self.bits[3:]
 
     def greet(self, devices):
         barrier = pltpu.get_barrier_semaphore()
@@ -203,7 +194,7 @@
     (flag, tokens, cotangent, query_bias, value_bias, expand_bias), refs = refs[:6], refs[6:]
     gains, refs = refs[:6], refs[6:]
     (wi_own, wo_own, we_own, ws_own), refs = refs[:4], refs[4:]
-    (rows_ref, cotangent_in, flag_in), refs = refs[:3], refs[3:]
+    (rows_low, cotangent_in, flag_in), refs = refs[:3], refs[3:]
     kept = [refs[STATES * layer : STATES * (layer + 1)] for layer in range(layers)]
     refs = refs[STATES * layers :]
     states = [refs[STATES * layer : STATES * (layer + 1)] for layer in range(layers)]
@@ -211,7 +202,7 @@
     tokens_in = states[0][16]
     biases = (query_bias, value_bias, expand_bias)
     biases_in, refs = refs[:3], refs[3:]
-    (save_sem, acc, rows_low, local_sem, send_sem, recv_sem, kv_send, kv_recv, misc_send, misc_recv) = refs
+    (save_sem, acc, local_sem, send_sem, recv_sem, kv_send, kv_recv, misc_send, misc_recv) = refs
     links = Links()
     core = links.core
     sems = (send_sem, recv_sem)
@@ -243,20 +234,16 @@
     swap_tokens = remote(tokens, tokens_in, misc, 0, links.opposite)
     swap_flag = remote(flag, flag_in, misc, 1, links.opposite)
     swap_cotangent = remote(cotangent, cotangent_in, misc, 2, links.opposite)
-    swap_rows = remote(rows_low, rows_ref, misc, 3, links.opposite)
     copy_biases = [remote(biases[number], biases_in[number], misc, 4 + number, links.across) for number in range(3)]
+
+    for copy in copy_biases:
+        copy.start()
+    every[0].start()
 
     @pl.when(links.moved)
     def _():
         swap_flag.start()
         swap_tokens.start()
-
-    for copy in copy_biases:
-        copy.start()
-    every[0].start()
-
-    @pl.when(links.moved)
-    def _():
         for weight in every[1:]:
             weight.start()
         swap_cotangent.start()
@@ -284,13 +271,16 @@
             lax.rem(index, 2) == 0, biases[number][layer : layer + 1, place], biases_in[number][layer : layer + 1, place]
         )
 
+    for copy in copy_biases:
+        copy.wait_recv()
+    every[0].relay()
+    every[0].relay_again()
+
     @pl.when(links.moved)
     def _():
         swap_flag.wait_recv()
         swap_tokens.wait_recv()
 
-    for copy in copy_biases:
-        copy.wait_recv()
     shift = jnp.where(flag_in[0:1, 0:1] < 0.5, 0.0, MASKED)
     acc[...] = tokens_in[...].astype(F32)
     halves = lane_halves((rows, width))
@@ -331,32 +321,33 @@
         after_pair = [[], [], [], []]
         if layer == 0:
             before_pair = [
-                [],
-                [wi_go.relay_again, wo_go.relay],
-                [wi_go.relay_last, wo_go.relay_again, we_go.relay, wi_go.wait_fetched, project_rest],
-                [wo_go.relay_last, we_go.relay_again, ws_go.relay],
+                [wi_go.relay_last],
+                [wo_go.relay, we_go.relay],
+                [wo_go.relay_again, we_go.relay_again, ws_go.relay, wi_go.wait_fetched, project_rest, wo_go.relay_last, wo_go.wait_fetched],
+                [ws_go.relay_again, we_go.relay_last],
             ]
-            after_pair[0] = [start_rest, wi_go.relay]
-            before_feed = [we_go.relay_last, ws_go.relay_again, wo_go.wait_fetched]
-            before_quarter = [[], [ws_go.relay_last], [we_go.wait_fetched, ws_go.wait_fetched], []]
-            if later:
-                before_feed += [later[0].relay]
-                before_quarter[1] += [later[0].relay_again, later[1].relay]
-                before_quarter[2] += [later[2].relay]
-                before_quarter[3] += [later[0].relay_last, later[1].relay_again]
-        else:
-            before_pair = [
-                [ws_go.relay, we_go.relay_again, wo_go.relay_last],
-                [ws_go.relay_again, we_go.relay_last],
-                [ws_go.relay_last, wi_go.wait_fetched, project_rest],
-                [],
-            ]
-            before_feed = [wo_go.wait_fetched]
+            after_pair[0] = [start_rest]
+            before_feed = [ws_go.relay_last]
             before_quarter = [[], [], [we_go.wait_fetched, ws_go.wait_fetched], []]
             if later:
                 before_feed += [later[0].relay, later[1].relay]
-                before_quarter[2] += [later[0].relay_again, later[1].relay_again, later[2].relay]
-                before_quarter[3] += [later[0].relay_last]
+                before_quarter[1] += [later[2].relay]
+                before_quarter[2] += [later[0].relay_again, later[1].relay_again]
+                before_quarter[3] += [later[3].relay]
+        else:
+            before_pair = [
+                [wi_go.relay_last, wo_go.relay_last, we_go.relay_again],
+                [ws_go.relay_again, we_go.relay_last],
+                [ws_go.relay_last, wi_go.wait_fetched, project_rest, wo_go.wait_fetched],
+                [],
+            ]
+            before_feed = []
+            before_quarter = [[], [], [we_go.wait_fetched, ws_go.wait_fetched], []]
+            if later:
+                before_feed += [later[0].relay, later[1].relay]
+                before_quarter[1] += [later[2].relay]
+                before_quarter[2] += [later[0].relay_again, later[1].relay_again]
+                before_quarter[3] += [later[3].relay]
         acc[...] += vector(0)
 
         def one_pair(step, carry):
@@ -385,16 +376,13 @@
             mixed_ref[index] = mixed_low
             totals = jnp.where(halves, total[0], total[1]).T
             total_ref[index] = jnp.concatenate([totals[0:8], totals[DH : DH + 8]], 0)
+            acc[...] += dot(mixed_low, wo[index])
             return carry
 
+        wo_go.wait_own()
         lax.fori_loop(0, 4, one_pair, 0)
         for action in before_feed:
             action()
-        wo_go.wait_own()
-        total = acc[...]
-        for index in range(4):
-            total = total + dot(mixed_ref[index], wo[index])
-        acc[...] = total
         save(layer, 16, 0, 4, 5, 6, 1, 7, 8)
         first, scale = normalise(acc[...])
         first_ref[...] = first
@@ -428,17 +416,8 @@
 
     @pl.when(links.moved)
     def _():
-        swap_rows.start()
-
-    @pl.when(jnp.logical_not(links.moved))
-    def _():
-        rows_ref[...] = rows_low[...]
-
-    @pl.when(links.moved)
-    def _():
-        for copy in (swap_cotangent, swap_rows):
-            copy.wait_recv()
-        for copy in (swap_tokens, swap_flag, swap_cotangent, swap_rows):
+        swap_cotangent.wait_recv()
+        for copy in (swap_tokens, swap_flag, swap_cotangent):
             copy.wait_send()
 
     for copy in copy_biases:
@@ -469,94 +448,96 @@
     return 3 - ordered(step)
 
 
-GRADIENT_LANES = (
-    ((1, 0, 4), (-1, 1, 4), (1, 2, 4), (-1, 3, 4)),
-    ((-1, 0, 1),),
-    ((1, 0, 3), (-1, 1, 3), (1, 2, 3)),
-)
-
-
-def lanes_of(kind, columns):
-    return [(way, at * columns // parts, columns // parts) for way, at, parts in GRADIENT_LANES[kind]]
-
-
 class Gradient:
-    def __init__(self, links, number, mine, theirs, core_in, narrow_in, slots, further_in, out, lanes, sems):
+    def __init__(self, links, number, mine, theirs, core_in, narrow_in, pair_in, line_in, further_in, out, sems):
         self.links, self.number, self.mine, self.theirs, self.core_in = links, number, mine, theirs, core_in
-        self.narrow_in, self.slots, self.further_in, self.out, self.lanes, self.sems = narrow_in, slots, further_in, out, lanes, sems
+        self.narrow_in, self.pair_in, self.line_in, self.further_in, self.out, self.sems = narrow_in, pair_in, line_in, further_in, out, sems
         self.size = core_in.shape[1]
-        self.piece = mine.shape[1] // links.chips
+        self.piece = mine.shape[1] // 8
+
+    def copy(self, source, target, at, device):
+        return remote(source, target, self.sems, (self.number, at), device)
 
     def part_copy(self, part):
-        return remote(self.theirs.at[part], self.core_in.at[part], self.sems[0], (self.number, part), self.links.beside)
+        return self.copy(self.theirs.at[part], self.core_in.at[part], part, self.links.beside)
 
     def narrow_copy(self):
-        return remote(self.mine.at[1, pl.ds(0, self.size)], self.narrow_in, self.sems[0], (self.number, 2), self.links.across)
+        return self.copy(self.mine.at[1, pl.ds(0, self.size)], self.narrow_in, 2, self.links.across)
 
     def share_copy(self):
         place = self.out.at[self.links.core]
-        return remote(place, place, self.sems[0], (self.number, 3), self.links.beside)
-
-    def ring_copy(self, lane, step):
-        links = self.links
-        way, at, count = self.lanes[lane]
-        device = links.right if way > 0 else links.left
-        where = (self.number, lane, step)
-        if step < links.chips - 1:
-            source = self.mine.at[0, self.rows(-way * step), pl.ds(at, count)]
-            return remote(source, self.slots[lane].at[step], self.sems[1], where, device)
-        rows = self.rows(-way * (step - links.chips))
-        target = self.out.at[links.core, rows, pl.ds(at, count)]
-        source = self.mine.at[0, rows, pl.ds(at, count)] if step == links.chips - 1 else target
-        return remote(source, target, self.sems[1], where, device)
-
-    def further_copy(self, lane, number):
-        way, at, count = self.lanes[lane]
-        source = self.mine.at[0, self.rows(way), pl.ds(at, count)]
-        return remote(source, self.further_in[lane].at[number], self.sems[2], (self.number, lane, number), self.links.further[number])
-
-    def rows(self, offset):
-        index = lax.rem(self.links.place + offset + 2 * self.links.chips, self.links.chips)
+        return self.copy(place, place, 3, self.links.beside)
+
+    def half_rows(self, other):
+        bit = self.links.bit + other * (1 - 2 * self.links.bit)
+        return pl.ds(pl.multiple_of(bit * 4 * self.piece, 16), 4 * self.piece)
+
+    def piece_rows(self, offset):
+        index = 4 * self.links.bit + lax.rem(self.links.line + offset, 4)
         return pl.ds(pl.multiple_of(index * self.piece, 16), self.piece)
+
+    def pair_copy(self):
+        return self.copy(self.mine.at[0, self.half_rows(1)], self.pair_in, 4, self.links.along)
+
+    def line_copy(self, offset):
+        device = self.links.line_peers[offset - 1]
+        return self.copy(self.mine.at[0, self.piece_rows(offset)], self.line_in.at[offset - 1], 4 + offset, device)
+
+    def line_back(self, offset):
+        place = self.out.at[self.links.core, self.piece_rows(0)]
+        return self.copy(place, place, 7 + offset, self.links.line_peers[offset - 1])
+
+    def pair_back(self):
+        place = self.out.at[self.links.core, self.half_rows(0)]
+        return self.copy(place, place, 11, self.links.along)
+
+    def further_copy(self, number):
+        place = self.mine.at[0, self.piece_rows(0)]
+        return self.copy(place, self.further_in.at[number], 12 + number, self.links.further[number])
 
     def send(self, part):
         self.part_copy(part).start()
 
     def middle(self):
         self.part_copy(1).wait_recv()
-        total = self.mine[1, 0 : self.size].astype(F32) + self.core_in[1].astype(F32)
-        self.mine[1, 0 : self.size] = total.astype(BF16)
+        self.mine[1, 0 : self.size] = add(self.mine[1, 0 : self.size], self.core_in[1])
         self.narrow_copy().start()
 
     def settle(self):
         self.part_copy(0).wait_recv()
         self.narrow_copy().wait_recv()
-        total = self.mine[0, 0 : self.size].astype(F32) + self.core_in[0].astype(F32) + self.narrow_in[...].astype(F32)
-        self.mine[0, 0 : self.size] = total.astype(BF16)
-        for lane in range(len(self.lanes)):
-            self.ring_copy(lane, 0).start()
-
-    def tick(self, step):
-        chips = self.links.chips
-        for lane, (way, at, count) in enumerate(self.lanes):
-            self.ring_copy(lane, step).wait_recv()
-            if step < chips - 1:
-                rows = self.rows(-way * (step + 1))
-                total = self.mine[0, rows, at : at + count].astype(F32) + self.slots[lane][step].astype(F32)
-                total = total.astype(BF16)
-                self.mine[0, rows, at : at + count] = total
-                for number in range(len(self.links.further) if step == chips - 2 else 0):
-                    copy = self.further_copy(lane, number)
-                    copy.start()
-                    copy.wait()
-                    total = (total.astype(F32) + self.further_in[lane][number].astype(F32)).astype(BF16)
-                    self.mine[0, rows, at : at + count] = total
-                if step == chips - 2:
-                    self.out[self.links.core, rows, at : at + count] = total
-            if step < 2 * chips - 3:
-                self.ring_copy(lane, step + 1).start()
+        self.mine[0, 0 : self.size] = add(self.mine[0, 0 : self.size], self.core_in[0], self.narrow_in[...])
+        self.pair_copy().start()
+
+    def cross(self):
+        self.pair_copy().wait_recv()
+        rows = self.half_rows(0)
+        self.mine[0, rows] = add(self.mine[0, rows], self.pair_in[...])
+        for offset in range(1, 4):
+            self.line_copy(offset).start()
+
+    def spread(self):
+        for offset in range(1, 4):
+            self.line_copy(offset).wait_recv()
+        rows = self.piece_rows(0)
+        total = add(self.mine[0, rows], self.line_in[0], self.line_in[1], self.line_in[2])
+        for number in range(len(self.links.further)):
+            self.mine[0, rows] = total
+            copy = self.further_copy(number)
+            copy.start()
+            copy.wait()
+            total = add(total, self.further_in[number])
+        self.out[self.links.core, rows] = total
+        for offset in range(1, 4):
+            self.line_back(offset).start()
+
+    def widen(self):
+        for offset in range(1, 4):
+            self.line_back(offset).wait_recv()
+        self.pair_back().start()
 
     def share(self):
+        self.pair_back().wait_recv()
         self.share_copy().start()
 
     def free_theirs(self):
@@ -565,40 +546,43 @@
 
     def wait_all(self, theirs_waited):
         self.share_copy().wait_recv()
-        self.share_copy().wait_send()
         if not theirs_waited:
             self.free_theirs()
-        self.narrow_copy().wait_send()
-        for lane in range(len(self.lanes)):
-            for step in range(2 * self.links.chips - 2):
-                self.ring_copy(lane, step).wait_send()
+        copies = [self.share_copy(), self.narrow_copy(), self.pair_copy(), self.pair_back()]
+        for offset in range(1, 4):
+            copies += [self.line_copy(offset), self.line_back(offset)]
+        for copy in copies:
+            copy.wait_send()
+
+
+def add(*terms):
+    total = terms[0].astype(F32)
+    for term in terms[1:]:
+        total = total + term.astype(F32)
+    return total.astype(BF16)
 
 
 def all_backward(layers, chips, *refs):
-    (flag, cotangent), refs = refs[:2], refs[2:]
+    (flag, cotangent, out_low), refs = refs[:3], refs[3:]
     gains, refs = refs[:6], refs[6:]
     kept = [refs[STATES * layer : STATES * (layer + 1)] for layer in range(layers)]
     refs = refs[STATES * layers :]
-    (rows_ref, small_out), refs = refs[:2], refs[2:]
-    outs = [[ref.at[layer] for ref in refs[:3]] for layer in range(layers)]
-    refs = refs[3:]
+    (out_rows, rows_ref, small_out), refs = refs[:3], refs[3:]
+    outs = [[ref.at[layer] for ref in refs[:KINDS]] for layer in range(layers)]
+    refs = refs[KINDS:]
     state, refs = refs[:STATES], refs[STATES:]
-    (acc, turned, summed_ref, mixed_grad_ref, inner_ref, query_grad_ref, here_ref, away_ref, rows_low), refs = refs[:9], refs[9:]
+    (acc, turned, summed_ref, mixed_grad_ref, inner_ref, query_grad_ref, here_ref, away_ref, rows_low, rows_back), refs = refs[:10], refs[10:]
     away_in, refs = refs[:layers], refs[layers:]
-    theirs, refs = refs[:3], refs[3:]
+    theirs, refs = refs[:KINDS], refs[KINDS:]
     buffers = []
     for layer in range(layers):
-        group = []
-        for lanes in GRADIENT_LANES:
-            count = len(lanes)
-            group.append((refs[0], refs[1], refs[2], refs[3 : 3 + count], refs[3 + count : 3 + 2 * count]))
-            refs = refs[3 + 2 * count :]
-        buffers.append(group)
+        buffers.append([refs[6 * kind : 6 * kind + 6] for kind in range(KINDS)])
+        refs = refs[6 * KINDS :]
     (small, core_small, mid_small, row_small, sum_small, step_small), refs = refs[:6], refs[6:]
-    (load_sem, away_send, away_recv, grad_send, grad_recv, ring_send, ring_recv, misc_send, misc_recv, step_send, step_recv, further_send, further_recv) = refs
+    (load_sem, away_send, away_recv, grad_send, grad_recv, misc_send, misc_recv, step_send, step_recv) = refs
     (wi, wo, we, ws, query, pair, remote_pair, mixed, total_ref, normed, first, first_scale, active, slope, second, second_scale, hidden_low) = state
     links = Links()
-    links.ring(chips)
+    links.plane(chips)
     core = links.core
     steps = chips.bit_length() - 1
     bits = links.bits
@@ -618,16 +602,16 @@
     pair_group = (4, 5, 6, 8)
     input_group = (16, 0)
     load(layers - 1, block_group + pair_group + input_group)
-    links.greet([links.across, links.beside, links.opposite, links.right, links.left] + bits)
+    links.greet([links.across, links.beside, links.opposite] + links.line_peers + bits)
     misc = (misc_send, misc_recv)
     gradients = []
     for layer in range(layers):
         group = []
-        for kind in range(3):
-            mine, core_in, narrow_in, slots, further_in = buffers[layer][kind]
+        for kind in range(KINDS):
+            mine, core_in, narrow_in, pair_in, line_in, further_in = buffers[layer][kind]
             group.append(Gradient(
-                links, 3 * layer + kind, mine, theirs[kind], core_in, narrow_in, slots, further_in, outs[layer][kind],
-                lanes_of(kind, mine.shape[2]), ((grad_send, grad_recv), (ring_send, ring_recv), (further_send, further_recv)),
+                links, KINDS * layer + kind, mine, theirs[kind], core_in, narrow_in, pair_in, line_in, further_in,
+                outs[layer][kind], (grad_send, grad_recv),
             ))
         gradients.append(group)
     rows, width = mixed.shape[1], mixed.shape[2]
@@ -639,8 +623,19 @@
     which = lax.broadcasted_iota(jnp.int32, (16, width), 0) // 8
     selector = (half == which).astype(F32)
     acc[...] = cotangent[...].astype(F32)
+    swap_rows = remote(rows_back, rows_ref, misc, 0, links.opposite)
+    swap_out = remote(out_low, out_rows, misc, 4, links.opposite)
+
+    @pl.when(links.moved)
+    def _():
+        swap_out.start()
+
+    @pl.when(jnp.logical_not(links.moved))
+    def _():
+        out_rows[...] = out_low[...]
+
     for layer in reversed(range(layers)):
-        feed, output, inputs = gradients[layer]
+        shrink, expand, output, input_one, input_two = gradients[layer]
         before = gradients[layer + 1] if layer + 1 < layers else None
         vector = lambda at: gains[at][layer : layer + 1]
 
@@ -653,8 +648,8 @@
             def _():
                 gradient.theirs[index - 2, at : at + value.shape[0]] = value
 
-        def tick(kind, step):
-            return lambda: before[kind].tick(step)
+        def act(name, *which):
+            return [getattr(gradient, name) for gradient in which]
 
         loaded(layer, 14, 15)
         incoming = acc[...]
@@ -668,19 +663,18 @@
         if before:
             for gradient in before:
                 gradient.free_theirs()
-        block_hooks = [[], [functools.partial(feed.send, 1)], [], [functools.partial(feed.send, 0), feed.middle]]
+        partly = lambda part, *which: [functools.partial(gradient.send, part) for gradient in which]
+        block_hooks = [[], partly(1, shrink, expand), [], partly(0, shrink, expand) + act("middle", shrink, expand)]
         if before:
-            block_hooks[0].append(before[0].settle)
-            block_hooks[1].append(tick(0, 0))
-            block_hooks[3].append(tick(0, 1))
+            block_hooks[0] += act("cross", before[0]) + act("settle", before[1])
 
         def one_quarter(step, carry):
             at_step(step, block_hooks)
             index = backwards(step)
             branch = rows_low[...]
             inner = (dot_rt(branch, ws[index]) * slope[index].astype(F32)).astype(BF16)
-            put(feed, index, 0, dot_lt(active[index], branch).astype(BF16))
-            put(feed, index, units, dot(turned[...], inner).astype(BF16))
+            put(shrink, index, 0, dot_lt(active[index], branch).astype(BF16))
+            put(expand, index, 0, dot(turned[...], inner).astype(BF16))
             small[index, 8 * layer + 6 : 8 * layer + 7, 0:units] = column_sum(inner.astype(F32))
             acc[...] += dot_rt(inner, we[index])
             return carry
@@ -696,8 +690,8 @@
         summed_ref[...] = summed
         rows_low[...] = summed.astype(BF16)
         if before:
-            before[0].tick(2)
-            before[1].settle()
+            before[0].spread()
+            before[1].cross()
             before[2].settle()
 
         def one_output(step, carry):
@@ -718,16 +712,12 @@
             load(layer - 1, block_group)
         loaded(layer, *pair_group)
         pair_hooks = [[], [output.middle], [], []]
-        middle_hooks = [[], [], [], []]
         if before:
-            both = lambda step: [tick(1, step), tick(2, step)]
-            pair_hooks[0] += [tick(0, 3)] + both(0)
-            pair_hooks[1] += [tick(0, 4)] + both(1)
-            middle_hooks[1] += [tick(0, 5)] + both(2)
-            pair_hooks[2] += [tick(0, 6)] + both(3)
-            middle_hooks[2] += [tick(0, 7)] + both(4)
-            pair_hooks[3] += [tick(0, 8)] + both(5)
-            middle_hooks[3] += [tick(0, 9)] + both(6)
+            pair_hooks[0] += act("settle", before[3], before[4])
+            pair_hooks[1] += act("cross", before[2]) + act("widen", before[0])
+            pair_hooks[2] += act("spread", before[1], before[2])
+            pair_hooks[3] += act("cross", before[3], before[4])
+        pair_hooks[3] += act("settle", shrink)
 
         def away_copy(there):
             return remote(away_ref.at[there], away_in[layer].at[there], (away_send, away_recv), (layer, there), links.beside)
@@ -743,8 +733,6 @@
             queries, grads = query[index], mixed_grad_ref[index]
             query_turned = None
             for side in range(2):
-                if side == 1:
-                    at_step(step, middle_hooks)
                 source, place = (pair, index) if side == 0 else (remote_pair, there)
                 keys, values = source[place, :, :width], source[place, :, width:]
                 key_grad = value_grad = None
@@ -781,12 +769,10 @@
         loaded(layer, *input_group)
         turned[...] = hidden_low[...].T
         acc[...] = summed_ref[...]
-        input_hooks = [[], [functools.partial(inputs.send, 1)], [inputs.middle], [functools.partial(inputs.send, 0)]]
+        input_hooks = [[], partly(1, input_one, input_two), [], act("middle", input_one, input_two) + partly(0, input_one, input_two)]
         if before:
-            feed.settle()
-            input_hooks[0] += [tick(0, 10)] + both(7)
-            input_hooks[2] += [tick(0, 11)] + both(8)
-            input_hooks[3] += [functools.partial(feed.tick, 0)]
+            input_hooks[0] += act("share", before[0])
+            input_hooks[2] += act("widen", before[1], before[2])
 
         def one_input(step, carry):
             at_step(step, input_hooks)
@@ -794,7 +780,9 @@
             away_copy(index).wait_recv()
             pair_grad = (here_ref[index] + away_in[layer][index].astype(F32)).astype(BF16)
             triple = jnp.concatenate([query_grad_ref[index], pair_grad], 1)
-            put(inputs, index, 0, dot(turned[...], triple).astype(BF16))
+            update = dot(turned[...], triple).astype(BF16)
+            put(input_one, index, 0, update[: depth // 2])
+            put(input_two, index, 0, update[depth // 2 :])
             acc[...] += dot_rt(triple, wi[index])
             small[index, 8 * layer + 7 : 8 * layer + 8, 0 : 3 * width] = column_sum(triple.astype(F32))
             return carry
@@ -803,9 +791,8 @@
         if layer > 0:
             load(layer - 1, input_group)
 
-    feed, output, inputs = gradients[0]
-    rows_low[...] = acc[...].astype(BF16)
-    swap_rows = remote(rows_low, rows_ref, misc, 0, links.opposite)
+    shrink, expand, output, input_one, input_two = gradients[0]
+    rows_back[...] = acc[...].astype(BF16)
     copy_core = remote(small.at[pl.ds(2, 2)], core_small, misc, 1, links.beside)
     copy_row = remote(mid_small, row_small, misc, 2, links.across)
     share_small = remote(small_out.at[core], small_out.at[core], misc, 3, links.beside)
@@ -822,49 +809,53 @@
     def _():
         swap_rows.start()
 
-    ticks = 2 * links.chips - 2
-    queues = []
+    plan = [(shrink, "cross"), (expand, "settle")]
     if layers > 1:
-        queues += [(0, gradients[1][0], 12), (0, gradients[1][1], 9), (0, gradients[1][2], 9)]
-    late_at, small_at = 3, 4
-    started = 1
-    if layers == 1:
-        feed.settle()
-        started = 0
-    queues += [(0, feed, started), (1, output, 0), (late_at + 1, inputs, 0)]
-    value = None
-    for step in range(late_at + 1 + ticks):
+        shrink_two, expand_two, output_two, input_three, input_four = gradients[1]
+        plan = [(input_three, "spread"), (input_four, "spread")] + plan + [(expand_two, "share"), (output_two, "share")]
+    plan += [(output, "settle"), (shrink, "spread")]
+    if layers > 1:
+        plan += [(input_three, "widen"), (input_four, "widen")]
+    plan += [
+        (expand, "cross"), (output, "cross"), (input_one, "settle"), (shrink, "widen"), (expand, "spread"), (output, "spread"),
+        (input_one, "cross"), (input_two, "settle"),
+    ]
+    if layers > 1:
+        plan += [(input_three, "share"), (input_four, "share")]
+    plan += [
+        None, (shrink, "share"), (expand, "widen"), (input_one, "spread"), (input_two, "cross"), None, (output, "widen"),
+        (input_one, "widen"), None, (expand, "share"), (input_two, "spread"), (output, "share"), None, (input_one, "share"), (input_two, "widen"),
+    ]
+    plan += [None] * (steps - 3) + [(input_two, "share")]
+    step, value = 0, None
+    for entry in plan:
+        if entry:
+            getattr(entry[0], entry[1])()
+            continue
         if step == 0:
-            output.settle()
-        if step == late_at:
-            inputs.settle()
-        for start, gradient, done in queues:
-            at = step - start + done
-            if step >= start and at < ticks:
-                gradient.tick(at)
-                if at == ticks - 1:
-                    gradient.share()
-        if step == small_at:
             copy_row.wait_recv()
             value = small[0] + core_small[0] + row_small[...]
-        if small_at < step <= small_at + steps:
-            step_copy(step - small_at - 1).wait_recv()
-            value = value + step_small[step - small_at - 1]
-        if small_at <= step < small_at + steps:
-            sum_small[step - small_at] = value
-            step_copy(step - small_at).start()
-        if step == small_at + steps:
+        else:
+            step_copy(step - 1).wait_recv()
+            value = value + step_small[step - 1]
+        if step < steps:
+            sum_small[step] = value
+            step_copy(step).start()
+        else:
             small_out[core] = value
             share_small.start()
+        step += 1
+    assert step == steps + 1
 
     @pl.when(links.moved)
     def _():
-        swap_rows.wait_recv()
-        swap_rows.wait_send()
+        for copy in (swap_rows, swap_out):
+            copy.wait_recv()
+            copy.wait_send()
 
     @pl.when(jnp.logical_not(links.moved))
     def _():
-        rows_ref[...] = rows_low[...]
+        rows_ref[...] = rows_back[...]
 
     share_small.wait_recv()
     share_small.wait_send()
@@ -880,15 +871,17 @@
 
 
 def assemble_kernel(layers, *refs):
-    (feed, output, inputs, small, out_rows, in_rows), refs = refs[:6], refs[6:]
+    (shrink, expand, output, input_one, input_two, small, out_rows, in_rows), refs = refs[:8], refs[8:]
     (shrink_ref, expand_ref, output_ref, input_ref, out_rows_ref, in_rows_ref), refs = refs[:6], refs[6:]
     vector_refs, (expand_bias_ref, query_bias_ref, value_bias_ref) = refs[:6], refs[6:]
     units, depth, width = shrink_ref.shape[1], shrink_ref.shape[2], output_ref.shape[1]
-    shrink_ref[0] = feed[0, 0, 0:units].astype(F32)
-    expand_ref[0] = feed[0, 0, units : units + depth].astype(F32)
+    shrink_ref[0] = shrink[0, 0, 0:units].astype(F32)
+    expand_ref[0] = expand[0, 0, 0:depth].astype(F32)
     output_ref[0] = output[0, 0, 0:width].astype(F32)
     for kind in range(3):
-        input_ref[0, kind] = inputs[0, 0, 0:depth, kind * width : (kind + 1) * width].astype(F32)
+        columns = slice(kind * width, (kind + 1) * width)
+        input_ref[0, kind, 0 : depth // 2] = input_one[0, 0, 0 : depth // 2, columns].astype(F32)
+        input_ref[0, kind, depth // 2 :] = input_two[0, 0, 0 : depth // 2, columns].astype(F32)
     out_rows_ref[...] = out_rows[...].astype(F32)
     in_rows_ref[...] = in_rows[...].astype(F32)
 
@@ -954,7 +947,7 @@
         out_specs=[VM] * 3 + [AN] * len(kept_shapes),
         scratch_shapes=state_scratch * layers + [pltpu.VMEM(bias.shape, F32) for bias in biases] + [
             pltpu.SemaphoreType.DMA((layers, STATES)),
-            pltpu.VMEM((rows, depth), F32), pltpu.VMEM((rows, depth), BF16),
+            pltpu.VMEM((rows, depth), F32),
             pltpu.SemaphoreType.DMA((4 * layers, 6)),
             pltpu.SemaphoreType.DMA((4 * layers, 10)), pltpu.SemaphoreType.DMA((4 * layers, 10)),
             pltpu.SemaphoreType.DMA((layers, 4)), pltpu.SemaphoreType.DMA((layers, 4)),
@@ -964,51 +957,47 @@
         cost_estimate=cost(10**10, 10**8),
         name="forward",
     )(flag, tokens, cotangent, *biases, *gains, input_own, output_own, expand_weight, shrink_own)
-    out_rows, cotangent, flag = results[:3]
+    out_low, cotangent, flag = results[:3]
     chips = wide // 2
-    ring = ring_size(chips)
-    further = (chips // ring).bit_length() - 1
-    tall = lambda size: -(-size // (16 * ring)) * 16 * ring
+    further = (chips // 8).bit_length() - 1
+    tall = lambda size: -(-size // 128) * 128
     out_shapes, buffer_scratch, theirs_scratch = [], [], []
-    for kind, (size, columns) in enumerate(((units + depth, depth), (width, depth), (depth, 3 * width))):
+    for size, columns in ((units, depth), (depth, units), (width, depth), (depth // 2, 3 * width), (depth // 2, 3 * width)):
         out_shapes.append(shaped(BF16, layers, 2, tall(size), columns))
         theirs_scratch.append(pltpu.VMEM((2, size, columns), BF16))
-        slot = lambda count: pltpu.VMEM((ring - 1, tall(size) // ring, count), BF16)
-        more = lambda count: pltpu.VMEM((further, tall(size) // ring, count) if further else (1, 16, 128), BF16)
+        piece = tall(size) // 8
         buffer_scratch += [
             pltpu.VMEM((2, tall(size), columns), BF16), pltpu.VMEM((2, size, columns), BF16), pltpu.VMEM((size, columns), BF16),
+            pltpu.VMEM((4 * piece, columns), BF16), pltpu.VMEM((3, piece, columns), BF16),
+            pltpu.VMEM((further, piece, columns) if further else (1, 16, 128), BF16),
         ]
-        lanes = lanes_of(kind, columns)
-        buffer_scratch += [slot(count) for way, at, count in lanes] + [more(count) for way, at, count in lanes]
     small_rows = 8 * layers
     steps = chips.bit_length() - 1
     small_scratch = pltpu.VMEM((small_rows, depth), F32)
-    ring_sem = pltpu.SemaphoreType.DMA((3 * layers, 4, 2 * ring - 2))
-    further_sem = pltpu.SemaphoreType.DMA((3 * layers, 4, max(further, 1)))
+    grad_sem = pltpu.SemaphoreType.DMA((KINDS * layers, 12 + further))
     results = pl.pallas_call(
         functools.partial(all_backward, layers, chips),
-        out_shape=[low_shape, shaped(F32, 2, small_rows, depth)] + out_shapes,
-        in_specs=[VM] * 8 + [AN] * len(kept_shapes),
-        out_specs=[VM] * 5,
+        out_shape=[low_shape, low_shape, shaped(F32, 2, small_rows, depth)] + out_shapes,
+        in_specs=[VM] * 9 + [AN] * len(kept_shapes),
+        out_specs=[VM] * (3 + KINDS),
         scratch_shapes=state_scratch + [
             pltpu.VMEM((rows, depth), F32), pltpu.VMEM((depth, rows), BF16), pltpu.VMEM((rows, depth), F32),
             pltpu.VMEM(query_shape.shape, BF16), pltpu.VMEM(stat_shape.shape, F32), pltpu.VMEM(query_shape.shape, BF16),
-            pltpu.VMEM(pair_shape.shape, F32), pltpu.VMEM(pair_shape.shape, BF16), pltpu.VMEM((rows, depth), BF16),
+            pltpu.VMEM(pair_shape.shape, F32), pltpu.VMEM(pair_shape.shape, BF16), pltpu.VMEM((rows, depth), BF16), pltpu.VMEM((rows, depth), BF16),
         ] + [pltpu.VMEM(pair_shape.shape, BF16)] * layers + theirs_scratch + buffer_scratch * layers + [
             pltpu.VMEM((4, small_rows, depth), F32), pltpu.VMEM((2, small_rows, depth), F32), small_scratch, small_scratch,
             pltpu.VMEM((steps, small_rows, depth), F32), pltpu.VMEM((steps, small_rows, depth), F32),
             pltpu.SemaphoreType.DMA((STATES,)),
             pltpu.SemaphoreType.DMA((layers, 4)), pltpu.SemaphoreType.DMA((layers, 4)),
-            pltpu.SemaphoreType.DMA((3 * layers, 4)), pltpu.SemaphoreType.DMA((3 * layers, 4)),
-            ring_sem, ring_sem,
-            pltpu.SemaphoreType.DMA((4,)), pltpu.SemaphoreType.DMA((4,)),
-            pltpu.SemaphoreType.DMA((steps,)), pltpu.SemaphoreType.DMA((steps,)), further_sem, further_sem,
+            grad_sem, grad_sem,
+            pltpu.SemaphoreType.DMA((5,)), pltpu.SemaphoreType.DMA((5,)),
+            pltpu.SemaphoreType.DMA((steps,)), pltpu.SemaphoreType.DMA((steps,)),
         ],
         compiler_params=pltpu.CompilerParams(collective_id=0, has_side_effects=True, vmem_limit_bytes=67043328),
         cost_estimate=cost(10**10, 10**8),
         name="backward",
-    )(flag, cotangent, *gains, *results[3:])
-    in_rows, small = results[:2]
+    )(flag, cotangent, out_low, *gains, *results[3:])
+    out_rows, in_rows, small = results[:3]
     whole = lambda *dims: pl.BlockSpec(dims, lambda layer, part: (0,) * len(dims))
     piece = lambda shape: pl.BlockSpec((1, 1) + shape.shape[2:], lambda layer, part: (layer, part, 0, 0))
     strip = pl.BlockSpec((rows // (2 * layers), depth), lambda layer, part: (2 * layer + part, 0))
@@ -1029,7 +1018,7 @@
         compiler_params=pltpu.CompilerParams(vmem_limit_bytes=40 * 2**20),
         cost_estimate=cost(10**6, 2 * 10**7),
         name="assemble",
-    )(*results[2:], small, out_rows, in_rows)
+    )(*results[3:], small, out_rows, in_rows)
     shrink_grad, expand_grad, output_grad, input_grad, layer_output, input_rows = outs[:6]
     second_shift_grad, second_gain_grad, shrink_bias_grad, first_shift_grad, first_gain_grad, output_bias_grad = outs[6:12]
     expand_bias_grad, query_bias_grad, value_bias_grad = outs[12:]

time: 255 us -> 221 us (0.87)
  Pallas kernels: 245 us -> 209 us
    pallas_call x1, Pallas kernels: 154 us -> 131 us  [local(): pl.pallas_call(functools.partial(all_backward, layers, chips), out_shape=...]
    pallas_call x1, Pallas kernels: 85.4 us -> 72.9 us  [local(): pl.pallas_call(functools.partial(all_forward, layers), out_shape=[low_sha...]
    unnamed x12 -> x16, local copies, waits for them, and re-layouts: 7.55 us -> 9.4 us
where the time goes in v2:
time: 221 us
  Pallas kernels  209 us (95%)
  local copies, waits for them, and re-layouts  10 us (5%)
    pallas_call x1, Pallas kernels, local(): pl.pallas_call(functools.partial(all_backward, layers, chips), out_shape=...  131 us
    pallas_call x1, Pallas kernels, local(): pl.pallas_call(functools.partial(all_forward, layers), out_shape=[low_sha...  72.9 us
    unnamed x16, local copies, waits for them, and re-layouts  9.4 us
    pallas_call x1, Pallas kernels, local(): pl.pallas_call(functools.partial(assemble_kernel, layers), grid=(layers,...  5.47 us

profile of v2, /device:TPU:0, one launch (start us, length us, event | category | flops | bytes accessed | tf_op | source)
XLA Modules:
  0.0 220.7 jit_solution(13833836208452483168)
XLA Ops:
  1.3 0.6 broadcast_in_dim.2.refs_0_
  1.9 72.9 %forward.1 = (bf16[512,512]{1,0:T(8,128)(2,1)}, bf16[512,512]{1,0:T(8,128)(2,1)}, f32[8,128]{1,0:T(8,128)}, bf16[4,512,384]{2,1,0:T(8,128)(2,1)}, bf16[4,128,512...) custom-call(f32[8,128]{1,0:T(8,128)} %broadcast_in_dim.2.refs_0_, ...), custom_call_target="tpu_custom_call" | custom-call | flops 10000000000 | bytes 100000000 | tf_op jit(solution)/shard_map/forward/pallas_call | solution.py:943
  74.8 130.9 %backward.1 = (bf16[512,512]{1,0:T(8,128)(2,1)}, bf16[512,512]{1,0:T(8,128)(2,1)}, f32[2,16,512]{2,1,0:T(8,128)}, bf16[2,2,512,512]{3,2,1,0:T(8,128)(2,1)}, bf16...) custom-call(f32[8,128]{1,0:T(8,128)} %get-tuple-element.75.refs_0_, ...), custom_call_target="tpu_custom_call" | custom-call | flops 10000000000 | bytes 100000000 | tf_op jit(solution)/shard_map/backward/pallas_call | solution.py:978
  205.7 0.0 copy-start
  205.7 1.6 copy-done
  207.2 0.0 copy-start.1
  207.2 1.6 copy-done.1
  208.8 0.0 copy-start.2
  208.8 1.1 copy-done.2
  210.0 0.0 copy-start.3
  210.0 1.1 copy-done.3
  211.1 0.0 copy-start.4
  211.1 1.0 copy-done.4
  212.1 0.0 copy-start.5
  212.1 1.0 copy-done.5
  213.2 0.0 copy-start.6
  213.2 1.0 copy-done.6
  214.2 0.0 copy-start.7
  214.2 0.8 copy-done.7
  215.1 5.5 %assemble.1 = (f32[2,1024,512]{2,1,0:T(8,128)}, f32[2,512,1024]{2,1,0:T(8,128)}, f32[2,256,512]{2,1,0:T(8,128)}, f32[2,3,512,256]{3,2,1,0:T(8,128)}, f32[512,512...) custom-call(bf16[2,2,512,512]{3,2,1,0:T(8,128)(2,1)S(1)} %copy-done,, ...), custom_call_target="tpu_custom_call" | custom-call | flops 1000000 | bytes 20000000 | tf_op jit(solution)/shard_map/assemble/pallas_call | solution.py:1006
Async XLA Ops:
  205.7 1.6 copy-start
  207.2 1.6 copy-start.1
  208.8 1.1 copy-start.2
  210.0 1.1 copy-start.3
  211.1 1.0 copy-start.4
  212.1 1.0 copy-start.5
  213.2 1.0 copy-start.6
  214.2 0.8 copy-start.7

commit v3 on v2

--- a/solution.py
+++ b/solution.py
@@ -1,4 +1,5 @@
 import functools
+import itertools
 
 import jax
 import jax.numpy as jnp
@@ -194,7 +195,7 @@
     (flag, tokens, cotangent, query_bias, value_bias, expand_bias), refs = refs[:6], refs[6:]
     gains, refs = refs[:6], refs[6:]
     (wi_own, wo_own, we_own, ws_own), refs = refs[:4], refs[4:]
-    (rows_low, cotangent_in, flag_in), refs = refs[:3], refs[3:]
+    (rows_out, cotangent_out, flag_out), refs = refs[:3], refs[3:]
     kept = [refs[STATES * layer : STATES * (layer + 1)] for layer in range(layers)]
     refs = refs[STATES * layers :]
     states = [refs[STATES * layer : STATES * (layer + 1)] for layer in range(layers)]
@@ -202,7 +203,7 @@
     tokens_in = states[0][16]
     biases = (query_bias, value_bias, expand_bias)
     biases_in, refs = refs[:3], refs[3:]
-    (save_sem, acc, local_sem, send_sem, recv_sem, kv_send, kv_recv, misc_send, misc_recv) = refs
+    (save_sem, pass_sem, rows_low, cotangent_in, flag_in, acc, local_sem, send_sem, recv_sem, kv_send, kv_recv, misc_send, misc_recv) = refs
     links = Links()
     core = links.core
     sems = (send_sem, recv_sem)
@@ -239,25 +240,25 @@
     for copy in copy_biases:
         copy.start()
     every[0].start()
+    every[1].start()
 
     @pl.when(links.moved)
     def _():
         swap_flag.start()
         swap_tokens.start()
-        for weight in every[1:]:
+        for weight in every[2:]:
             weight.start()
         swap_cotangent.start()
 
     @pl.when(jnp.logical_not(links.moved))
     def _():
         tokens_in[...] = tokens[...]
-        cotangent_in[...] = cotangent[...]
         flag_in[...] = flag[...]
 
     def start_rest():
         @pl.when(jnp.logical_not(links.moved))
         def _():
-            for weight in every[1:]:
+            for weight in every[2:]:
                 weight.start()
 
         for weight in every[4:]:
@@ -274,7 +275,9 @@
     for copy in copy_biases:
         copy.wait_recv()
     every[0].relay()
+    every[1].relay()
     every[0].relay_again()
+    every[1].relay_again()
 
     @pl.when(links.moved)
     def _():
@@ -291,6 +294,22 @@
     def save(layer, *numbers):
         for number in numbers:
             save_copy(layer, number).start()
+
+    pass_rows = pltpu.make_async_copy(rows_low, rows_out, pass_sem.at[0])
+    pass_flag = pltpu.make_async_copy(flag_in, flag_out, pass_sem.at[1])
+    pass_far = pltpu.make_async_copy(cotangent_in, cotangent_out, pass_sem.at[2])
+    pass_near = pltpu.make_async_copy(cotangent, cotangent_out, pass_sem.at[2])
+    pass_flag.start()
+
+    @pl.when(jnp.logical_not(links.moved))
+    def _():
+        pass_near.start()
+
+    def pass_cotangent():
+        @pl.when(links.moved)
+        def _():
+            swap_cotangent.wait_recv()
+            pass_far.start()
 
     for layer in range(layers):
         (wi, wo, we, ws, query_ref, pair_ref, remote_ref, mixed_ref, total_ref, normed_ref, first_ref, first_scale, active_ref, slope_ref, second_ref, second_scale, low_ref) = states[layer]
@@ -317,18 +336,19 @@
             lax.fori_loop(2, 4, project, 0)
 
         wi_go.wait_own()
+        if layer == 0:
+            start_rest()
         lax.fori_loop(0, 2, project, 0)
         after_pair = [[], [], [], []]
         if layer == 0:
             before_pair = [
-                [wi_go.relay_last],
-                [wo_go.relay, we_go.relay],
-                [wo_go.relay_again, we_go.relay_again, ws_go.relay, wi_go.wait_fetched, project_rest, wo_go.relay_last, wo_go.wait_fetched],
-                [ws_go.relay_again, we_go.relay_last],
+                [],
+                [wi_go.relay_last, wo_go.relay_last, we_go.relay],
+                [ws_go.relay, wi_go.wait_fetched, wo_go.wait_fetched, project_rest, we_go.relay_again],
+                [ws_go.relay_again],
             ]
-            after_pair[0] = [start_rest]
-            before_feed = [ws_go.relay_last]
-            before_quarter = [[], [], [we_go.wait_fetched, ws_go.wait_fetched], []]
+            before_feed = [we_go.relay_last]
+            before_quarter = [[], [ws_go.relay_last], [we_go.wait_fetched, ws_go.wait_fetched], []]
             if later:
                 before_feed += [later[0].relay, later[1].relay]
                 before_quarter[1] += [later[2].relay]
@@ -348,6 +368,9 @@
                 before_quarter[1] += [later[2].relay]
                 before_quarter[2] += [later[0].relay_again, later[1].relay_again]
                 before_quarter[3] += [later[3].relay]
+        before_quarter[3] += [functools.partial(save, layer, 2, 3)]
+        if not later:
+            before_quarter[3] += [pass_cotangent]
         acc[...] += vector(0)
 
         def one_pair(step, carry):
@@ -405,7 +428,7 @@
             return carry
 
         lax.fori_loop(0, 4, one_quarter, 0)
-        save(layer, 2, 3, 12, 13)
+        save(layer, 12, 13)
         second, scale = normalise(acc[...])
         second_ref[...] = second
         second_scale[...] = scale
@@ -413,10 +436,11 @@
         acc[...] = second * vector(4) + vector(5)
 
     rows_low[...] = acc[...].astype(BF16)
+    pass_rows.start()
 
     @pl.when(links.moved)
     def _():
-        swap_cotangent.wait_recv()
+        pass_far.wait()
         for copy in (swap_tokens, swap_flag, swap_cotangent):
             copy.wait_send()
 
@@ -427,6 +451,13 @@
     for layer in range(layers):
         for number in range(STATES):
             save_copy(layer, number).wait()
+    pass_rows.wait()
+    pass_flag.wait()
+
+    @pl.when(jnp.logical_not(links.moved))
+    def _():
+        pass_near.wait()
+
     for layer in range(layers):
         pair_ref, remote_ref = states[layer][5:7]
         for index in range(4):
@@ -448,12 +479,18 @@
     return 3 - ordered(step)
 
 
+def late_sum(layer, kind):
+    return False
+
+
 class Gradient:
-    def __init__(self, links, number, mine, theirs, core_in, narrow_in, pair_in, line_in, further_in, out, sems):
+    def __init__(self, links, number, late, mine, theirs, core_in, narrow_in, pair_in, line_in, further_in, out, sems):
         self.links, self.number, self.mine, self.theirs, self.core_in = links, number, mine, theirs, core_in
         self.narrow_in, self.pair_in, self.line_in, self.further_in, self.out, self.sems = narrow_in, pair_in, line_in, further_in, out, sems
         self.size = core_in.shape[1]
         self.piece = mine.shape[1] // 8
+        self.late = late
+        self.kept = (0, 1) if late else (0,)
 
     def copy(self, source, target, at, device):
         return remote(source, target, self.sems, (self.number, at), device)
@@ -462,7 +499,8 @@
         return self.copy(self.theirs.at[part], self.core_in.at[part], part, self.links.beside)
 
     def narrow_copy(self):
-        return self.copy(self.mine.at[1, pl.ds(0, self.size)], self.narrow_in, 2, self.links.across)
+        rows = self.piece_rows(0) if self.late else pl.ds(0, self.size)
+        return self.copy(self.mine.at[1, rows], self.narrow_in, 2, self.links.across)
 
     def share_copy(self):
         place = self.out.at[self.links.core]
@@ -476,12 +514,13 @@
         index = 4 * self.links.bit + lax.rem(self.links.line + offset, 4)
         return pl.ds(pl.multiple_of(index * self.piece, 16), self.piece)
 
-    def pair_copy(self):
-        return self.copy(self.mine.at[0, self.half_rows(1)], self.pair_in, 4, self.links.along)
-
-    def line_copy(self, offset):
+    def pair_copy(self, part):
+        return self.copy(self.mine.at[part, self.half_rows(1)], self.pair_in.at[part], 12 + part, self.links.along)
+
+    def line_copy(self, part, offset):
         device = self.links.line_peers[offset - 1]
-        return self.copy(self.mine.at[0, self.piece_rows(offset)], self.line_in.at[offset - 1], 4 + offset, device)
+        source = self.mine.at[part, self.piece_rows(offset)]
+        return self.copy(source, self.line_in.at[part, offset - 1], 13 + 3 * part + offset, device)
 
     def line_back(self, offset):
         place = self.out.at[self.links.core, self.piece_rows(0)]
@@ -493,34 +532,56 @@
 
     def further_copy(self, number):
         place = self.mine.at[0, self.piece_rows(0)]
-        return self.copy(place, self.further_in.at[number], 12 + number, self.links.further[number])
+        return self.copy(place, self.further_in.at[number], 20 + number, self.links.further[number])
 
     def send(self, part):
         self.part_copy(part).start()
 
     def middle(self):
-        self.part_copy(1).wait_recv()
-        self.mine[1, 0 : self.size] = add(self.mine[1, 0 : self.size], self.core_in[1])
-        self.narrow_copy().start()
+        if not self.late:
+            self.part_copy(1).wait_recv()
+            self.mine[1, 0 : self.size] = add(self.mine[1, 0 : self.size], self.core_in[1])
+            self.narrow_copy().start()
 
     def settle(self):
-        self.part_copy(0).wait_recv()
+        if self.late:
+            for part in range(2):
+                self.part_copy(part).wait_recv()
+                self.mine[part, 0 : self.size] = add(self.mine[part, 0 : self.size], self.core_in[part])
+                self.pair_copy(part).start()
+        else:
+            self.part_copy(0).wait_recv()
+            self.narrow_copy().wait_recv()
+            self.mine[0, 0 : self.size] = add(self.mine[0, 0 : self.size], self.core_in[0], self.narrow_in[...])
+            self.pair_copy(0).start()
+
+    def cross(self):
+        rows = self.half_rows(0)
+        for part in self.kept:
+            self.pair_copy(part).wait_recv()
+            self.mine[part, rows] = add(self.mine[part, rows], self.pair_in[part])
+            for offset in range(1, 4):
+                self.line_copy(part, offset).start()
+
+    def spread(self):
+        rows = self.piece_rows(0)
+        for part in reversed(self.kept):
+            for offset in range(1, 4):
+                self.line_copy(part, offset).wait_recv()
+            total = add(self.mine[part, rows], self.line_in[part, 0], self.line_in[part, 1], self.line_in[part, 2])
+            if self.late:
+                self.mine[part, rows] = total
+                if part == 1:
+                    self.narrow_copy().start()
+        if not self.late:
+            self.spread_total(total)
+
+    def fold(self):
         self.narrow_copy().wait_recv()
-        self.mine[0, 0 : self.size] = add(self.mine[0, 0 : self.size], self.core_in[0], self.narrow_in[...])
-        self.pair_copy().start()
-
-    def cross(self):
-        self.pair_copy().wait_recv()
-        rows = self.half_rows(0)
-        self.mine[0, rows] = add(self.mine[0, rows], self.pair_in[...])
-        for offset in range(1, 4):
-            self.line_copy(offset).start()
-
-    def spread(self):
-        for offset in range(1, 4):
-            self.line_copy(offset).wait_recv()
+        self.spread_total(add(self.mine[0, self.piece_rows(0)], self.narrow_in[...]))
+
+    def spread_total(self, total):
         rows = self.piece_rows(0)
-        total = add(self.mine[0, rows], self.line_in[0], self.line_in[1], self.line_in[2])
         for number in range(len(self.links.further)):
             self.mine[0, rows] = total
             copy = self.further_copy(number)
@@ -548,9 +609,11 @@
         self.share_copy().wait_recv()
         if not theirs_waited:
             self.free_theirs()
-        copies = [self.share_copy(), self.narrow_copy(), self.pair_copy(), self.pair_back()]
+        copies = [self.share_copy(), self.narrow_copy(), self.pair_back()]
         for offset in range(1, 4):
-            copies += [self.line_copy(offset), self.line_back(offset)]
+            copies.append(self.line_back(offset))
+            copies += [self.line_copy(part, offset) for part in self.kept]
+        copies += [self.pair_copy(part) for part in self.kept]
         for copy in copies:
             copy.wait_send()
 
@@ -563,7 +626,7 @@
 
 
 def all_backward(layers, chips, *refs):
-    (flag, cotangent, out_low), refs = refs[:3], refs[3:]
+    passed, refs = refs[:3], refs[3:]
     gains, refs = refs[:6], refs[6:]
     kept = [refs[STATES * layer : STATES * (layer + 1)] for layer in range(layers)]
     refs = refs[STATES * layers :]
@@ -579,7 +642,7 @@
         buffers.append([refs[6 * kind : 6 * kind + 6] for kind in range(KINDS)])
         refs = refs[6 * KINDS :]
     (small, core_small, mid_small, row_small, sum_small, step_small), refs = refs[:6], refs[6:]
-    (load_sem, away_send, away_recv, grad_send, grad_recv, misc_send, misc_recv, step_send, step_recv) = refs
+    (out_low, cotangent, flag, pass_sem, load_sem, away_send, away_recv, grad_send, grad_recv, misc_send, misc_recv, step_send, step_recv) = refs
     (wi, wo, we, ws, query, pair, remote_pair, mixed, total_ref, normed, first, first_scale, active, slope, second, second_scale, hidden_low) = state
     links = Links()
     links.plane(chips)
@@ -601,7 +664,10 @@
     block_group = (14, 15, 3, 13, 12, 2, 9, 10, 11, 1, 7)
     pair_group = (4, 5, 6, 8)
     input_group = (16, 0)
-    load(layers - 1, block_group + pair_group + input_group)
+    passes = [pltpu.make_async_copy(passed[number], (out_low, cotangent, flag)[number], pass_sem.at[number]) for number in range(3)]
+    passes[1].start()
+    passes[2].start()
+    load(layers - 1, block_group[:7])
     links.greet([links.across, links.beside, links.opposite] + links.line_peers + bits)
     misc = (misc_send, misc_recv)
     gradients = []
@@ -610,29 +676,36 @@
         for kind in range(KINDS):
             mine, core_in, narrow_in, pair_in, line_in, further_in = buffers[layer][kind]
             group.append(Gradient(
-                links, KINDS * layer + kind, mine, theirs[kind], core_in, narrow_in, pair_in, line_in, further_in,
+                links, KINDS * layer + kind, late_sum(layer, kind), mine, theirs[kind], core_in, narrow_in, pair_in, line_in, further_in,
                 outs[layer][kind], (grad_send, grad_recv),
             ))
         gradients.append(group)
     rows, width = mixed.shape[1], mixed.shape[2]
     units, depth = ws.shape[1], ws.shape[2]
     halves = lane_halves((rows, width))
+    passes[2].wait()
     shift = jnp.where(flag[0:1, 0:1] < 0.5, 0.0, MASKED)
     small[...] = jnp.zeros(small.shape, F32)
     half = lax.broadcasted_iota(jnp.int32, (16, width), 1) // DH
     which = lax.broadcasted_iota(jnp.int32, (16, width), 0) // 8
     selector = (half == which).astype(F32)
+    passes[1].wait()
     acc[...] = cotangent[...].astype(F32)
+    passes[0].start()
+    load(layers - 1, block_group[7:] + pair_group + input_group)
     swap_rows = remote(rows_back, rows_ref, misc, 0, links.opposite)
     swap_out = remote(out_low, out_rows, misc, 4, links.opposite)
 
-    @pl.when(links.moved)
-    def _():
-        swap_out.start()
-
-    @pl.when(jnp.logical_not(links.moved))
-    def _():
-        out_rows[...] = out_low[...]
+    def start_out():
+        passes[0].wait()
+
+        @pl.when(links.moved)
+        def _():
+            swap_out.start()
+
+        @pl.when(jnp.logical_not(links.moved))
+        def _():
+            out_rows[...] = out_low[...]
 
     for layer in reversed(range(layers)):
         shrink, expand, output, input_one, input_two = gradients[layer]
@@ -666,7 +739,8 @@
         partly = lambda part, *which: [functools.partial(gradient.send, part) for gradient in which]
         block_hooks = [[], partly(1, shrink, expand), [], partly(0, shrink, expand) + act("middle", shrink, expand)]
         if before:
-            block_hooks[0] += act("cross", before[0]) + act("settle", before[1])
+            block_hooks[0] += act("cross", before[0])
+            block_hooks[2] += act("settle", before[1])
 
         def one_quarter(step, carry):
             at_step(step, block_hooks)
@@ -691,8 +765,9 @@
         rows_low[...] = summed.astype(BF16)
         if before:
             before[0].spread()
-            before[1].cross()
             before[2].settle()
+        if shrink.late:
+            shrink.settle()
 
         def one_output(step, carry):
             index = backwards(step)
@@ -713,11 +788,12 @@
         loaded(layer, *pair_group)
         pair_hooks = [[], [output.middle], [], []]
         if before:
-            pair_hooks[0] += act("settle", before[3], before[4])
-            pair_hooks[1] += act("cross", before[2]) + act("widen", before[0])
-            pair_hooks[2] += act("spread", before[1], before[2])
-            pair_hooks[3] += act("cross", before[3], before[4])
-        pair_hooks[3] += act("settle", shrink)
+            pair_hooks[0] += act("settle", before[3], before[4]) + act("cross", before[1])
+            pair_hooks[1] += act("cross", before[2])
+            pair_hooks[2] += act("widen", before[0]) + act("cross", before[3], before[4])
+            pair_hooks[3] += act("spread", before[1], before[2])
+        else:
+            pair_hooks[3] += act("settle", shrink)
 
         def away_copy(there):
             return remote(away_ref.at[there], away_in[layer].at[there], (away_send, away_recv), (layer, there), links.beside)
@@ -771,8 +847,8 @@
         acc[...] = summed_ref[...]
         input_hooks = [[], partly(1, input_one, input_two), [], act("middle", input_one, input_two) + partly(0, input_one, input_two)]
         if before:
-            input_hooks[0] += act("share", before[0])
-            input_hooks[2] += act("widen", before[1], before[2])
+            input_hooks[0] += act("settle", shrink)
+            input_hooks[3] += act("share", before[0])
 
         def one_input(step, carry):
             at_step(step, input_hooks)
@@ -805,32 +881,29 @@
     mid_small[...] = small[1] + core_small[1]
     copy_row.start()
 
-    @pl.when(links.moved)
-    def _():
-        swap_rows.start()
-
-    plan = [(shrink, "cross"), (expand, "settle")]
-    if layers > 1:
-        shrink_two, expand_two, output_two, input_three, input_four = gradients[1]
-        plan = [(input_three, "spread"), (input_four, "spread")] + plan + [(expand_two, "share"), (output_two, "share")]
-    plan += [(output, "settle"), (shrink, "spread")]
-    if layers > 1:
-        plan += [(input_three, "widen"), (input_four, "widen")]
-    plan += [
-        (expand, "cross"), (output, "cross"), (input_one, "settle"), (shrink, "widen"), (expand, "spread"), (output, "spread"),
-        (input_one, "cross"), (input_two, "settle"),
+    assert layers == 2
+    shrink_two, expand_two, output_two, input_three, input_four = gradients[1]
+    plan = [
+        (expand_two, "widen"), (output_two, "widen"), (input_three, "spread"), (input_four, "spread"), (shrink, "cross"),
+        (expand, "settle"), (expand_two, "share"), (output_two, "share"), (input_three, "widen"), (input_four, "widen"),
+        (shrink, "spread"), (output, "settle"), (expand, "cross"), (input_one, "settle"), (input_two, "settle"), (output, "cross"),
+        (input_three, "share"), (input_four, "share"), None, (input_one, "cross"), (shrink, "widen"), (expand, "spread"),
+        (input_two, "cross"), (output, "spread"), None, (input_one, "spread"), (shrink, "share"), (input_two, "spread"),
+        (expand, "widen"), (input_one, "widen"), None, (output, "widen"), (input_two, "widen"), (expand, "share"), (output, "share"),
     ]
-    if layers > 1:
-        plan += [(input_three, "share"), (input_four, "share")]
-    plan += [
-        None, (shrink, "share"), (expand, "widen"), (input_one, "spread"), (input_two, "cross"), None, (output, "widen"),
-        (input_one, "widen"), None, (expand, "share"), (input_two, "spread"), (output, "share"), None, (input_one, "share"), (input_two, "widen"),
-    ]
-    plan += [None] * (steps - 3) + [(input_two, "share")]
+    plan += [None] * (steps - 2) + [(input_one, "share"), (input_two, "share")]
+    def start_rows():
+        @pl.when(links.moved)
+        def _():
+            swap_rows.start()
+
     step, value = 0, None
     for entry in plan:
         if entry:
             getattr(entry[0], entry[1])()
+            if entry == (input_one, "settle"):
+                start_out()
+                start_rows()
             continue
         if step == 0:
             copy_row.wait_recv()
@@ -944,9 +1017,10 @@
         functools.partial(all_forward, layers),
         out_shape=[low_shape, low_shape, shaped(F32, 8, 128)] + kept_shapes,
         in_specs=[VM] * 12 + [AN] * 4,
-        out_specs=[VM] * 3 + [AN] * len(kept_shapes),
+        out_specs=[AN] * (3 + len(kept_shapes)),
         scratch_shapes=state_scratch * layers + [pltpu.VMEM(bias.shape, F32) for bias in biases] + [
-            pltpu.SemaphoreType.DMA((layers, STATES)),
+            pltpu.SemaphoreType.DMA((layers, STATES)), pltpu.SemaphoreType.DMA((3,)),
+            pltpu.VMEM((rows, depth), BF16), pltpu.VMEM((rows, depth), BF16), pltpu.VMEM((8, 128), F32),
             pltpu.VMEM((rows, depth), F32),
             pltpu.SemaphoreType.DMA((4 * layers, 6)),
             pltpu.SemaphoreType.DMA((4 * layers, 10)), pltpu.SemaphoreType.DMA((4 * layers, 10)),
@@ -957,36 +1031,39 @@
         cost_estimate=cost(10**10, 10**8),
         name="forward",
     )(flag, tokens, cotangent, *biases, *gains, input_own, output_own, expand_weight, shrink_own)
-    out_low, cotangent, flag = results[:3]
     chips = wide // 2
     further = (chips // 8).bit_length() - 1
     tall = lambda size: -(-size // 128) * 128
-    out_shapes, buffer_scratch, theirs_scratch = [], [], []
-    for size, columns in ((units, depth), (depth, units), (width, depth), (depth // 2, 3 * width), (depth // 2, 3 * width)):
-        out_shapes.append(shaped(BF16, layers, 2, tall(size), columns))
-        theirs_scratch.append(pltpu.VMEM((2, size, columns), BF16))
+    sizes = ((units, depth), (depth, units), (width, depth), (depth // 2, 3 * width), (depth // 2, 3 * width))
+    out_shapes = [shaped(BF16, layers, 2, tall(size), columns) for size, columns in sizes]
+    theirs_scratch = [pltpu.VMEM((2, size, columns), BF16) for size, columns in sizes]
+    buffer_scratch = []
+    for layer, (kind, (size, columns)) in itertools.product(range(layers), enumerate(sizes)):
         piece = tall(size) // 8
+        late = late_sum(layer, kind)
+        kept = 2 if late else 1
         buffer_scratch += [
-            pltpu.VMEM((2, tall(size), columns), BF16), pltpu.VMEM((2, size, columns), BF16), pltpu.VMEM((size, columns), BF16),
-            pltpu.VMEM((4 * piece, columns), BF16), pltpu.VMEM((3, piece, columns), BF16),
+            pltpu.VMEM((2, tall(size), columns), BF16), pltpu.VMEM((2, size, columns), BF16), pltpu.VMEM((piece if late else size, columns), BF16),
+            pltpu.VMEM((kept, 4 * piece, columns), BF16), pltpu.VMEM((kept, 3, piece, columns), BF16),
             pltpu.VMEM((further, piece, columns) if further else (1, 16, 128), BF16),
         ]
     small_rows = 8 * layers
     steps = chips.bit_length() - 1
     small_scratch = pltpu.VMEM((small_rows, depth), F32)
-    grad_sem = pltpu.SemaphoreType.DMA((KINDS * layers, 12 + further))
+    grad_sem = pltpu.SemaphoreType.DMA((KINDS * layers, 20 + further))
     results = pl.pallas_call(
         functools.partial(all_backward, layers, chips),
         out_shape=[low_shape, low_shape, shaped(F32, 2, small_rows, depth)] + out_shapes,
-        in_specs=[VM] * 9 + [AN] * len(kept_shapes),
+        in_specs=[AN] * 3 + [VM] * 6 + [AN] * len(kept_shapes),
         out_specs=[VM] * (3 + KINDS),
         scratch_shapes=state_scratch + [
             pltpu.VMEM((rows, depth), F32), pltpu.VMEM((depth, rows), BF16), pltpu.VMEM((rows, depth), F32),
             pltpu.VMEM(query_shape.shape, BF16), pltpu.VMEM(stat_shape.shape, F32), pltpu.VMEM(query_shape.shape, BF16),
             pltpu.VMEM(pair_shape.shape, F32), pltpu.VMEM(pair_shape.shape, BF16), pltpu.VMEM((rows, depth), BF16), pltpu.VMEM((rows, depth), BF16),
-        ] + [pltpu.VMEM(pair_shape.shape, BF16)] * layers + theirs_scratch + buffer_scratch * layers + [
+        ] + [pltpu.VMEM(pair_shape.shape, BF16)] * layers + theirs_scratch + buffer_scratch + [
             pltpu.VMEM((4, small_rows, depth), F32), pltpu.VMEM((2, small_rows, depth), F32), small_scratch, small_scratch,
             pltpu.VMEM((steps, small_rows, depth), F32), pltpu.VMEM((steps, small_rows, depth), F32),
+            pltpu.VMEM((rows, depth), BF16), pltpu.VMEM((rows, depth), BF16), pltpu.VMEM((8, 128), F32), pltpu.SemaphoreType.DMA((3,)),
             pltpu.SemaphoreType.DMA((STATES,)),
             pltpu.SemaphoreType.DMA((layers, 4)), pltpu.SemaphoreType.DMA((layers, 4)),
             grad_sem, grad_sem,
@@ -996,7 +1073,7 @@
         compiler_params=pltpu.CompilerParams(collective_id=0, has_side_effects=True, vmem_limit_bytes=67043328),
         cost_estimate=cost(10**10, 10**8),
         name="backward",
-    )(flag, cotangent, out_low, *gains, *results[3:])
+    )(*results[:3], *gains, *results[3:])
     out_rows, in_rows, small = results[:3]
     whole = lambda *dims: pl.BlockSpec(dims, lambda layer, part: (0,) * len(dims))
     piece = lambda shape: pl.BlockSpec((1, 1) + shape.shape[2:], lambda layer, part: (layer, part, 0, 0))
@@ -1015,7 +1092,7 @@
             upright(units), pl.BlockSpec((1, depth, units), lambda layer, part: (layer, 0, part)), upright(width),
             pl.BlockSpec((1, 3, depth, width), lambda layer, part: (layer, 0, 0, part)), strip, strip,
         ] + [whole(layers, depth)] * 6 + [whole(layers, 2 * units), whole(layers, 2 * width), whole(layers, 2 * width)],
-        compiler_params=pltpu.CompilerParams(vmem_limit_bytes=40 * 2**20),
+        compiler_params=pltpu.CompilerParams(vmem_limit_bytes=67043328),
         cost_estimate=cost(10**6, 2 * 10**7),
         name="assemble",
     )(*results[3:], small, out_rows, in_rows)

time: 221 us -> 206 us (0.932)
  local copies, waits for them, and re-layouts: 10 us -> 0.6 us
  Pallas kernels: 209 us -> 202 us
    unnamed x16 -> x0, local copies, waits for them, and re-layouts: 9.4 us -> none
    pallas_call x1, Pallas kernels: 72.9 us -> 67.2 us  [local(): pl.pallas_call(functools.partial(all_forward, layers), out_shape=[low_sha...]
    pallas_call x1, Pallas kernels: 131 us -> 126 us  [local(): pl.pallas_call(functools.partial(all_backward, layers, chips), out_shape=...]
    pallas_call x1, Pallas kernels: 5.47 us -> 9.01 us  [local(): pl.pallas_call(functools.partial(assemble_kernel, layers), grid=(layers,...]
where the time goes in v3:
time: 206 us; the launch traced here: 204 us
  Pallas kernels  202 us (98%)
    pallas_call x1, Pallas kernels, local(): pl.pallas_call(functools.partial(all_backward, layers, chips), out_shape=...  126 us
    pallas_call x1, Pallas kernels, local(): pl.pallas_call(functools.partial(all_forward, layers), out_shape=[low_sha...  67.2 us
    pallas_call x1, Pallas kernels, local(): pl.pallas_call(functools.partial(assemble_kernel, layers), grid=(layers,...  9.01 us

profile of v3, /device:TPU:0, one launch (start us, length us, event | category | flops | bytes accessed | tf_op | source)
XLA Modules:
  0.0 203.8 jit_solution(5845761370516374880)
XLA Ops:
  1.3 0.6 broadcast_in_dim.2.refs_0_
  1.9 67.2 %forward.1 = (bf16[512,512]{1,0:T(8,128)(2,1)}, bf16[512,512]{1,0:T(8,128)(2,1)}, f32[8,128]{1,0:T(8,128)}, bf16[4,512,384]{2,1,0:T(8,128)(2,1)}, bf16[4,128,512...) custom-call(f32[8,128]{1,0:T(8,128)} %broadcast_in_dim.2.refs_0_, ...), custom_call_target="tpu_custom_call" | custom-call | flops 10000000000 | bytes 100000000 | tf_op jit(solution)/shard_map/forward/pallas_call | solution.py:1016
  69.1 125.5 %backward.1 = (bf16[512,512]{1,0:T(8,128)(2,1)}, bf16[512,512]{1,0:T(8,128)(2,1)}, f32[2,16,512]{2,1,0:T(8,128)}, bf16[2,2,512,512]{3,2,1,0:T(8,128)(2,1)}, bf16...) custom-call(bf16[512,512]{1,0:T(8,128)(2,1)} %get-tuple-element.75.r, ...), custom_call_target="tpu_custom_call" | custom-call | flops 10000000000 | bytes 100000000 | tf_op jit(solution)/shard_map/backward/pallas_call | solution.py:1054
  194.6 9.0 %assemble.1 = (f32[2,1024,512]{2,1,0:T(8,128)}, f32[2,512,1024]{2,1,0:T(8,128)}, f32[2,256,512]{2,1,0:T(8,128)}, f32[2,3,512,256]{3,2,1,0:T(8,128)}, f32[512,512...) custom-call(bf16[2,2,512,512]{3,2,1,0:T(8,128)(2,1)} %get-tuple-elem, ...), custom_call_target="tpu_custom_call" | custom-call | flops 1000000 | bytes 20000000 | tf_op jit(solution)/shard_map/assemble/pallas_call | solution.py:1083

commit v4 on v3

--- a/solution.py
+++ b/solution.py
@@ -83,10 +83,12 @@
         self.further = self.bits[3:]
 
     def greet(self, devices):
-        barrier = pltpu.get_barrier_semaphore()
+        self.greeted = len(devices)
         for device in devices:
-            pl.semaphore_signal(barrier, inc=1, device_id=device, device_id_type=pl.DeviceIdType.MESH)
-        pl.semaphore_wait(barrier, len(devices))
+            pl.semaphore_signal(pltpu.get_barrier_semaphore(), inc=1, device_id=device, device_id_type=pl.DeviceIdType.MESH)
+
+    def wait_greetings(self):
+        pl.semaphore_wait(pltpu.get_barrier_semaphore(), self.greeted)
 
 
 def remote(source, target, sems, at, device):
@@ -113,22 +115,26 @@
         for slot, part in ((0, core), (2, 1 - core)):
             for kind in range(self.parts):
                 target = self.buffer.at[slot, :, pl.ds(kind * self.columns, self.columns)]
-                copies.append(pltpu.make_async_copy(self.own(part, slice(None), kind), target, self.local_sem.at[self.number, len(copies)]))
+                at = 12 * (self.number // 4) + (0 if self.parts > 1 else 4 + 2 * (self.number % 4)) + len(copies)
+                copies.append(pltpu.make_async_copy(self.own(part, slice(None), kind), target, self.local_sem.at[at]))
         return copies
+
+    def place(self, at):
+        return 34 * (self.number // 4) + (at if self.parts > 1 else 8 * (self.number % 4) + 2 + at)
 
     def first_hops(self):
         rows = self.rows(0, 0)
         return [
             remote(
                 self.own(self.links.core, rows, kind), self.buffer.at[1, rows, pl.ds(kind * self.columns, self.columns)],
-                self.sems, (self.number, kind), self.links.across,
+                self.sems, self.place(kind), self.links.across,
             )
             for kind in range(self.parts)
         ]
 
     def hop(self, kind):
         links = self.links
-        at = (self.number, 2 + kind)
+        at = self.place(self.parts - 1 + kind)
         device = links.along if kind == 1 or (kind == 3 and self.number % 2) else links.along_next
         if kind < 3:
             rows = self.rows(0, 0)
@@ -192,7 +198,7 @@
 
 
 def all_forward(layers, *refs):
-    (flag, tokens, cotangent, query_bias, value_bias, expand_bias), refs = refs[:6], refs[6:]
+    (bucket, tokens, cotangent, query_bias, value_bias, expand_bias), refs = refs[:6], refs[6:]
     gains, refs = refs[:6], refs[6:]
     (wi_own, wo_own, we_own, ws_own), refs = refs[:4], refs[4:]
     (rows_out, cotangent_out, flag_out), refs = refs[:3], refs[3:]
@@ -203,7 +209,7 @@
     tokens_in = states[0][16]
     biases = (query_bias, value_bias, expand_bias)
     biases_in, refs = refs[:3], refs[3:]
-    (save_sem, pass_sem, rows_low, cotangent_in, flag_in, acc, local_sem, send_sem, recv_sem, kv_send, kv_recv, misc_send, misc_recv) = refs
+    (save_sem, pass_sem, rows_low, cotangent_in, flag_in, flag_own, acc, local_sem, send_sem, recv_sem, kv_send, kv_recv, misc_send, misc_recv) = refs
     links = Links()
     core = links.core
     sems = (send_sem, recv_sem)
@@ -228,14 +234,23 @@
             for number in range(4)
         ])
     every = [weight for group in weights for weight in group]
+    links.greet([links.across, links.along, links.along_next, links.beside, links.opposite])
+    fill_tokens = pltpu.make_async_copy(tokens, tokens_in, pass_sem.at[2])
+
+    @pl.when(jnp.logical_not(links.moved))
+    def _():
+        fill_tokens.start()
+
     for weight in every[:4]:
         weight.start_local()
-    links.greet([links.across, links.along, links.along_next, links.beside, links.opposite])
+    flag = flag_own
+    flag[...] = jnp.full(flag.shape, bucket[0], jnp.int32).astype(F32)
+    links.wait_greetings()
     misc = (misc_send, misc_recv)
     swap_tokens = remote(tokens, tokens_in, misc, 0, links.opposite)
     swap_flag = remote(flag, flag_in, misc, 1, links.opposite)
     swap_cotangent = remote(cotangent, cotangent_in, misc, 2, links.opposite)
-    copy_biases = [remote(biases[number], biases_in[number], misc, 4 + number, links.across) for number in range(3)]
+    copy_biases = [remote(biases[number], biases_in[number], misc, 3 + number, links.across) for number in range(3)]
 
     for copy in copy_biases:
         copy.start()
@@ -252,7 +267,7 @@
 
     @pl.when(jnp.logical_not(links.moved))
     def _():
-        tokens_in[...] = tokens[...]
+        fill_tokens.wait()
         flag_in[...] = flag[...]
 
     def start_rest():
@@ -298,12 +313,7 @@
     pass_rows = pltpu.make_async_copy(rows_low, rows_out, pass_sem.at[0])
     pass_flag = pltpu.make_async_copy(flag_in, flag_out, pass_sem.at[1])
     pass_far = pltpu.make_async_copy(cotangent_in, cotangent_out, pass_sem.at[2])
-    pass_near = pltpu.make_async_copy(cotangent, cotangent_out, pass_sem.at[2])
     pass_flag.start()
-
-    @pl.when(jnp.logical_not(links.moved))
-    def _():
-        pass_near.start()
 
     def pass_cotangent():
         @pl.when(links.moved)
@@ -454,10 +464,6 @@
     pass_rows.wait()
     pass_flag.wait()
 
-    @pl.when(jnp.logical_not(links.moved))
-    def _():
-        pass_near.wait()
-
     for layer in range(layers):
         pair_ref, remote_ref = states[layer][5:7]
         for index in range(4):
@@ -479,18 +485,13 @@
     return 3 - ordered(step)
 
 
-def late_sum(layer, kind):
-    return False
-
-
 class Gradient:
-    def __init__(self, links, number, late, mine, theirs, core_in, narrow_in, pair_in, line_in, further_in, out, sems):
+    def __init__(self, links, number, mine, theirs, core_in, narrow_in, pair_in, line_in, further_in, out, result, result_sem, sems):
+        self.result, self.result_sem, self.collected = result, result_sem, False
         self.links, self.number, self.mine, self.theirs, self.core_in = links, number, mine, theirs, core_in
         self.narrow_in, self.pair_in, self.line_in, self.further_in, self.out, self.sems = narrow_in, pair_in, line_in, further_in, out, sems
         self.size = core_in.shape[1]
         self.piece = mine.shape[1] // 8
-        self.late = late
-        self.kept = (0, 1) if late else (0,)
 
     def copy(self, source, target, at, device):
         return remote(source, target, self.sems, (self.number, at), device)
@@ -499,8 +500,7 @@
         return self.copy(self.theirs.at[part], self.core_in.at[part], part, self.links.beside)
 
     def narrow_copy(self):
-        rows = self.piece_rows(0) if self.late else pl.ds(0, self.size)
-        return self.copy(self.mine.at[1, rows], self.narrow_in, 2, self.links.across)
+        return self.copy(self.mine.at[1, pl.ds(0, self.size)], self.narrow_in, 2, self.links.across)
 
     def share_copy(self):
         place = self.out.at[self.links.core]
@@ -514,13 +514,12 @@
         index = 4 * self.links.bit + lax.rem(self.links.line + offset, 4)
         return pl.ds(pl.multiple_of(index * self.piece, 16), self.piece)
 
-    def pair_copy(self, part):
-        return self.copy(self.mine.at[part, self.half_rows(1)], self.pair_in.at[part], 12 + part, self.links.along)
-
-    def line_copy(self, part, offset):
+    def pair_copy(self):
+        return self.copy(self.mine.at[0, self.half_rows(1)], self.pair_in, 4, self.links.along)
+
+    def line_copy(self, offset):
         device = self.links.line_peers[offset - 1]
-        source = self.mine.at[part, self.piece_rows(offset)]
-        return self.copy(source, self.line_in.at[part, offset - 1], 13 + 3 * part + offset, device)
+        return self.copy(self.mine.at[0, self.piece_rows(offset)], self.line_in.at[offset - 1], 4 + offset, device)
 
     def line_back(self, offset):
         place = self.out.at[self.links.core, self.piece_rows(0)]
@@ -532,56 +531,34 @@
 
     def further_copy(self, number):
         place = self.mine.at[0, self.piece_rows(0)]
-        return self.copy(place, self.further_in.at[number], 20 + number, self.links.further[number])
+        return self.copy(place, self.further_in.at[number], 12 + number, self.links.further[number])
 
     def send(self, part):
         self.part_copy(part).start()
 
     def middle(self):
-        if not self.late:
-            self.part_copy(1).wait_recv()
-            self.mine[1, 0 : self.size] = add(self.mine[1, 0 : self.size], self.core_in[1])
-            self.narrow_copy().start()
+        self.part_copy(1).wait_recv()
+        self.mine[1, 0 : self.size] = add(self.mine[1, 0 : self.size], self.core_in[1])
+        self.narrow_copy().start()
 
     def settle(self):
-        if self.late:
-            for part in range(2):
-                self.part_copy(part).wait_recv()
-                self.mine[part, 0 : self.size] = add(self.mine[part, 0 : self.size], self.core_in[part])
-                self.pair_copy(part).start()
-        else:
-            self.part_copy(0).wait_recv()
-            self.narrow_copy().wait_recv()
-            self.mine[0, 0 : self.size] = add(self.mine[0, 0 : self.size], self.core_in[0], self.narrow_in[...])
-            self.pair_copy(0).start()
+        self.part_copy(0).wait_recv()
+        self.narrow_copy().wait_recv()
+        self.mine[0, 0 : self.size] = add(self.mine[0, 0 : self.size], self.core_in[0], self.narrow_in[...])
+        self.pair_copy().start()
 
     def cross(self):
         rows = self.half_rows(0)
-        for part in self.kept:
-            self.pair_copy(part).wait_recv()
-            self.mine[part, rows] = add(self.mine[part, rows], self.pair_in[part])
-            for offset in range(1, 4):
-                self.line_copy(part, offset).start()
+        self.pair_copy().wait_recv()
+        self.mine[0, rows] = add(self.mine[0, rows], self.pair_in[...])
+        for offset in range(1, 4):
+            self.line_copy(offset).start()
 
     def spread(self):
         rows = self.piece_rows(0)
-        for part in reversed(self.kept):
-            for offset in range(1, 4):
-                self.line_copy(part, offset).wait_recv()
-            total = add(self.mine[part, rows], self.line_in[part, 0], self.line_in[part, 1], self.line_in[part, 2])
-            if self.late:
-                self.mine[part, rows] = total
-                if part == 1:
-                    self.narrow_copy().start()
-        if not self.late:
-            self.spread_total(total)
-
-    def fold(self):
-        self.narrow_copy().wait_recv()
-        self.spread_total(add(self.mine[0, self.piece_rows(0)], self.narrow_in[...]))
-
-    def spread_total(self, total):
-        rows = self.piece_rows(0)
+        for offset in range(1, 4):
+            self.line_copy(offset).wait_recv()
+        total = add(self.mine[0, rows], self.line_in[0], self.line_in[1], self.line_in[2])
         for number in range(len(self.links.further)):
             self.mine[0, rows] = total
             copy = self.further_copy(number)
@@ -597,25 +574,39 @@
             self.line_back(offset).wait_recv()
         self.pair_back().start()
 
+    def result_copy(self, part):
+        return pltpu.make_async_copy(self.out.at[part], self.result.at[part], self.result_sem.at[self.number, part])
+
     def share(self):
         self.pair_back().wait_recv()
         self.share_copy().start()
+        self.result_copy(self.links.core).start()
+
+    def collect(self):
+        self.share_copy().wait_recv()
+        self.result_copy(1 - self.links.core).start()
+        self.collected = True
 
     def free_theirs(self):
         for part in range(2):
             self.part_copy(part).wait_send()
 
     def wait_all(self, theirs_waited):
-        self.share_copy().wait_recv()
+        if not self.collected:
+            self.collect()
         if not theirs_waited:
             self.free_theirs()
         copies = [self.share_copy(), self.narrow_copy(), self.pair_back()]
         for offset in range(1, 4):
             copies.append(self.line_back(offset))
-            copies += [self.line_copy(part, offset) for part in self.kept]
-        copies += [self.pair_copy(part) for part in self.kept]
+            copies.append(self.line_copy(offset))
+        copies.append(self.pair_copy())
         for copy in copies:
             copy.wait_send()
+
+    def wait_results(self):
+        for part in range(2):
+            self.result_copy(part).wait()
 
 
 def add(*terms):
@@ -626,13 +617,13 @@
 
 
 def all_backward(layers, chips, *refs):
-    passed, refs = refs[:3], refs[3:]
+    passed, cotangent_near, refs = refs[:3], refs[3], refs[4:]
     gains, refs = refs[:6], refs[6:]
     kept = [refs[STATES * layer : STATES * (layer + 1)] for layer in range(layers)]
     refs = refs[STATES * layers :]
     (out_rows, rows_ref, small_out), refs = refs[:3], refs[3:]
-    outs = [[ref.at[layer] for ref in refs[:KINDS]] for layer in range(layers)]
-    refs = refs[KINDS:]
+    results, refs = refs[:KINDS], refs[KINDS:]
+    outs, refs = refs[:KINDS], refs[KINDS:]
     state, refs = refs[:STATES], refs[STATES:]
     (acc, turned, summed_ref, mixed_grad_ref, inner_ref, query_grad_ref, here_ref, away_ref, rows_low, rows_back), refs = refs[:10], refs[10:]
     away_in, refs = refs[:layers], refs[layers:]
@@ -642,7 +633,7 @@
         buffers.append([refs[6 * kind : 6 * kind + 6] for kind in range(KINDS)])
         refs = refs[6 * KINDS :]
     (small, core_small, mid_small, row_small, sum_small, step_small), refs = refs[:6], refs[6:]
-    (out_low, cotangent, flag, pass_sem, load_sem, away_send, away_recv, grad_send, grad_recv, misc_send, misc_recv, step_send, step_recv) = refs
+    (result_sem, out_low, cotangent, flag, pass_sem, load_sem, away_send, away_recv, grad_send, grad_recv, misc_send, misc_recv, step_send, step_recv) = refs
     (wi, wo, we, ws, query, pair, remote_pair, mixed, total_ref, normed, first, first_scale, active, slope, second, second_scale, hidden_low) = state
     links = Links()
     links.plane(chips)
@@ -665,7 +656,16 @@
     pair_group = (4, 5, 6, 8)
     input_group = (16, 0)
     passes = [pltpu.make_async_copy(passed[number], (out_low, cotangent, flag)[number], pass_sem.at[number]) for number in range(3)]
-    passes[1].start()
+    near = pltpu.make_async_copy(cotangent_near, cotangent, pass_sem.at[1])
+
+    @pl.when(links.moved)
+    def _():
+        passes[1].start()
+
+    @pl.when(jnp.logical_not(links.moved))
+    def _():
+        near.start()
+
     passes[2].start()
     load(layers - 1, block_group[:7])
     links.greet([links.across, links.beside, links.opposite] + links.line_peers + bits)
@@ -676,8 +676,8 @@
         for kind in range(KINDS):
             mine, core_in, narrow_in, pair_in, line_in, further_in = buffers[layer][kind]
             group.append(Gradient(
-                links, KINDS * layer + kind, late_sum(layer, kind), mine, theirs[kind], core_in, narrow_in, pair_in, line_in, further_in,
-                outs[layer][kind], (grad_send, grad_recv),
+                links, KINDS * layer + kind, mine, theirs[kind], core_in, narrow_in, pair_in, line_in, further_in,
+                outs[kind].at[layer], results[kind].at[layer], result_sem, (grad_send, grad_recv),
             ))
         gradients.append(group)
     rows, width = mixed.shape[1], mixed.shape[2]
@@ -753,6 +753,8 @@
             acc[...] += dot_rt(inner, we[index])
             return carry
 
+        if not before:
+            links.wait_greetings()
         lax.fori_loop(0, 4, one_quarter, 0)
         loaded(layer, 10, 11, 1, 7)
         outgoing = acc[...]
@@ -766,8 +768,6 @@
         if before:
             before[0].spread()
             before[2].settle()
-        if shrink.late:
-            shrink.settle()
 
         def one_output(step, carry):
             index = backwards(step)
@@ -827,7 +827,7 @@
                     slopes = (weights * slopes).astype(BF16)
                     update = dot(slopes, masked_query)
                     key_grad = update if key_grad is None else key_grad + update
-                    update = dot_lt(masked_key, slopes)
+                    update = dot_lt(slopes, masked_key)
                     query_turned = update if query_turned is None else query_turned + update
                 if side == 0:
                     here_ref[index, :, :width] = key_grad
@@ -836,7 +836,7 @@
                     away_ref[there, :, :width] = key_grad.astype(BF16)
                     away_ref[there, :, width:] = value_grad.astype(BF16)
             away_copy(there).start()
-            query_grad_ref[index] = (query_turned * DH ** (-0.5)).T.astype(BF16)
+            query_grad_ref[index] = (query_turned * DH ** (-0.5)).astype(BF16)
             return carry
 
         lax.fori_loop(0, 4, one_pair, 0)
@@ -891,7 +891,7 @@
         (input_two, "cross"), (output, "spread"), None, (input_one, "spread"), (shrink, "share"), (input_two, "spread"),
         (expand, "widen"), (input_one, "widen"), None, (output, "widen"), (input_two, "widen"), (expand, "share"), (output, "share"),
     ]
-    plan += [None] * (steps - 2) + [(input_one, "share"), (input_two, "share")]
+    plan += [(gradient, "collect") for gradient in gradients[1]] + [None] * (steps - 2) + [(input_one, "share"), (input_two, "share")]
     def start_rows():
         @pl.when(links.moved)
         def _():
@@ -941,6 +941,9 @@
     for layer in range(layers):
         for gradient in gradients[layer]:
             gradient.wait_all(layer > 0)
+    for layer in range(layers):
+        for gradient in gradients[layer]:
+            gradient.wait_results()
 
 
 def assemble_kernel(layers, *refs):
@@ -973,6 +976,7 @@
 
 VM = pl.BlockSpec(memory_space=pltpu.VMEM)
 AN = pl.BlockSpec(memory_space=pl.ANY)
+SM = pl.BlockSpec(memory_space=pltpu.SMEM)
 
 
 def shaped(dtype, *dims):
@@ -994,7 +998,6 @@
     width = input_weight.shape[3] // 2
     units = expand_weight.shape[2] // 2
 
-    flag = jnp.broadcast_to(bucket, (8, 128)).astype(F32)
     input_own = input_weight.transpose(0, 2, 1, 3)
     output_own = output_weight.reshape(layers, 2, width, depth)
     shrink_own = shrink_weight.reshape(layers, 2, units, depth)
@@ -1016,21 +1019,21 @@
     results = pl.pallas_call(
         functools.partial(all_forward, layers),
         out_shape=[low_shape, low_shape, shaped(F32, 8, 128)] + kept_shapes,
-        in_specs=[VM] * 12 + [AN] * 4,
+        in_specs=[SM] + [AN] * 2 + [VM] * 9 + [AN] * 4,
         out_specs=[AN] * (3 + len(kept_shapes)),
         scratch_shapes=state_scratch * layers + [pltpu.VMEM(bias.shape, F32) for bias in biases] + [
             pltpu.SemaphoreType.DMA((layers, STATES)), pltpu.SemaphoreType.DMA((3,)),
-            pltpu.VMEM((rows, depth), BF16), pltpu.VMEM((rows, depth), BF16), pltpu.VMEM((8, 128), F32),
+            pltpu.VMEM((rows, depth), BF16), pltpu.VMEM((rows, depth), BF16), pltpu.VMEM((8, 128), F32), pltpu.VMEM((8, 128), F32),
             pltpu.VMEM((rows, depth), F32),
-            pltpu.SemaphoreType.DMA((4 * layers, 6)),
-            pltpu.SemaphoreType.DMA((4 * layers, 10)), pltpu.SemaphoreType.DMA((4 * layers, 10)),
+            pltpu.SemaphoreType.DMA((12 * layers,)),
+            pltpu.SemaphoreType.DMA((34 * layers,)), pltpu.SemaphoreType.DMA((34 * layers,)),
             pltpu.SemaphoreType.DMA((layers, 4)), pltpu.SemaphoreType.DMA((layers, 4)),
-            pltpu.SemaphoreType.DMA((7,)), pltpu.SemaphoreType.DMA((7,)),
+            pltpu.SemaphoreType.DMA((6,)), pltpu.SemaphoreType.DMA((6,)),
         ],
         compiler_params=pltpu.CompilerParams(collective_id=1, has_side_effects=True, vmem_limit_bytes=62 * 2**20),
         cost_estimate=cost(10**10, 10**8),
         name="forward",
-    )(flag, tokens, cotangent, *biases, *gains, input_own, output_own, expand_weight, shrink_own)
+    )(bucket, tokens, cotangent, *biases, *gains, input_own, output_own, expand_weight, shrink_own)
     chips = wide // 2
     further = (chips // 8).bit_length() - 1
     tall = lambda size: -(-size // 128) * 128
@@ -1040,29 +1043,28 @@
     buffer_scratch = []
     for layer, (kind, (size, columns)) in itertools.product(range(layers), enumerate(sizes)):
         piece = tall(size) // 8
-        late = late_sum(layer, kind)
-        kept = 2 if late else 1
         buffer_scratch += [
-            pltpu.VMEM((2, tall(size), columns), BF16), pltpu.VMEM((2, size, columns), BF16), pltpu.VMEM((piece if late else size, columns), BF16),
-            pltpu.VMEM((kept, 4 * piece, columns), BF16), pltpu.VMEM((kept, 3, piece, columns), BF16),
+            pltpu.VMEM((2, tall(size), columns), BF16), pltpu.VMEM((2, size, columns), BF16), pltpu.VMEM((size, columns), BF16),
+            pltpu.VMEM((4 * piece, columns), BF16), pltpu.VMEM((3, piece, columns), BF16),
             pltpu.VMEM((further, piece, columns) if further else (1, 16, 128), BF16),
         ]
     small_rows = 8 * layers
     steps = chips.bit_length() - 1
     small_scratch = pltpu.VMEM((small_rows, depth), F32)
-    grad_sem = pltpu.SemaphoreType.DMA((KINDS * layers, 20 + further))
+    grad_sem = pltpu.SemaphoreType.DMA((KINDS * layers, 12 + further))
     results = pl.pallas_call(
         functools.partial(all_backward, layers, chips),
         out_shape=[low_shape, low_shape, shaped(F32, 2, small_rows, depth)] + out_shapes,
-        in_specs=[AN] * 3 + [VM] * 6 + [AN] * len(kept_shapes),
-        out_specs=[VM] * (3 + KINDS),
-        scratch_shapes=state_scratch + [
+        in_specs=[AN] * 4 + [VM] * 6 + [AN] * len(kept_shapes),
+        out_specs=[VM] * 3 + [AN] * KINDS,
+        scratch_shapes=[pltpu.VMEM(shape.shape, BF16) for shape in out_shapes] + state_scratch + [
             pltpu.VMEM((rows, depth), F32), pltpu.VMEM((depth, rows), BF16), pltpu.VMEM((rows, depth), F32),
             pltpu.VMEM(query_shape.shape, BF16), pltpu.VMEM(stat_shape.shape, F32), pltpu.VMEM(query_shape.shape, BF16),
             pltpu.VMEM(pair_shape.shape, F32), pltpu.VMEM(pair_shape.shape, BF16), pltpu.VMEM((rows, depth), BF16), pltpu.VMEM((rows, depth), BF16),
         ] + [pltpu.VMEM(pair_shape.shape, BF16)] * layers + theirs_scratch + buffer_scratch + [
             pltpu.VMEM((4, small_rows, depth), F32), pltpu.VMEM((2, small_rows, depth), F32), small_scratch, small_scratch,
             pltpu.VMEM((steps, small_rows, depth), F32), pltpu.VMEM((steps, small_rows, depth), F32),
+            pltpu.SemaphoreType.DMA((KINDS * layers, 2)),
             pltpu.VMEM((rows, depth), BF16), pltpu.VMEM((rows, depth), BF16), pltpu.VMEM((8, 128), F32), pltpu.SemaphoreType.DMA((3,)),
             pltpu.SemaphoreType.DMA((STATES,)),
             pltpu.SemaphoreType.DMA((layers, 4)), pltpu.SemaphoreType.DMA((layers, 4)),
@@ -1073,7 +1075,7 @@
         compiler_params=pltpu.CompilerParams(collective_id=0, has_side_effects=True, vmem_limit_bytes=67043328),
         cost_estimate=cost(10**10, 10**8),
         name="backward",
-    )(*results[:3], *gains, *results[3:])
+    )(*results[:3], cotangent, *gains, *results[3:])
     out_rows, in_rows, small = results[:3]
     whole = lambda *dims: pl.BlockSpec(dims, lambda layer, part: (0,) * len(dims))
     piece = lambda shape: pl.BlockSpec((1, 1) + shape.shape[2:], lambda layer, part: (layer, part, 0, 0))

time: 206 us -> 202 us (0.981)
  Pallas kernels: 202 us -> 198 us
    pallas_call x1, Pallas kernels: 126 us -> 123 us  [local(): pl.pallas_call(functools.partial(all_backward, layers, chips), out_shape=...]
where the time goes in v4:
time: 202 us; the launch traced here: 200 us
  Pallas kernels  198 us (98%)
    pallas_call x1, Pallas kernels, local(): pl.pallas_call(functools.partial(all_backward, layers, chips), out_shape=...  123 us
    pallas_call x1, Pallas kernels, local(): pl.pallas_call(functools.partial(all_forward, layers), out_shape=[low_sha...  66.4 us
    pallas_call x1, Pallas kernels, local(): pl.pallas_call(functools.partial(assemble_kernel, layers), grid=(layers,...  9.01 us

profile of v4, /device:TPU:0, one launch (start us, length us, event | category | flops | bytes accessed | tf_op | source)
XLA Modules:
  0.0 199.7 jit_solution(7011300582475240935)
XLA Ops:
  1.3 66.4 %forward.1 = (bf16[512,512]{1,0:T(8,128)(2,1)}, bf16[512,512]{1,0:T(8,128)(2,1)}, f32[8,128]{1,0:T(8,128)}, bf16[4,512,384]{2,1,0:T(8,128)(2,1)}, bf16[4,128,512...) custom-call(s32[1]{0:T(128)S(6)} %copy.31.refs_0_, ...), custom_call_target="tpu_custom_call" | custom-call | flops 10000000000 | bytes 100000000 | tf_op jit(solution)/shard_map/forward/pallas_call | solution.py:1019
  67.7 122.8 %backward.1 = (bf16[512,512]{1,0:T(8,128)(2,1)}, bf16[512,512]{1,0:T(8,128)(2,1)}, f32[2,16,512]{2,1,0:T(8,128)}, bf16[2,2,512,512]{3,2,1,0:T(8,128)(2,1)}, bf16...) custom-call(bf16[512,512]{1,0:T(8,128)(2,1)} %get-tuple-element.75.r, ...), custom_call_target="tpu_custom_call" | custom-call | flops 10000000000 | bytes 100000000 | tf_op jit(solution)/shard_map/backward/pallas_call | solution.py:1055
  190.5 9.0 %assemble.1 = (f32[2,1024,512]{2,1,0:T(8,128)}, f32[2,512,1024]{2,1,0:T(8,128)}, f32[2,256,512]{2,1,0:T(8,128)}, f32[2,3,512,256]{3,2,1,0:T(8,128)}, f32[512,512...) custom-call(bf16[2,2,512,512]{3,2,1,0:T(8,128)(2,1)} %get-tuple-elem, ...), custom_call_target="tpu_custom_call" | custom-call | flops 1000000 | bytes 20000000 | tf_op jit(solution)/shard_map/assemble/pallas_call | solution.py:1085
